TPU v7x, 32 devices: a whole 2x2x4 slice. The times are simulated.
32 devices in a mesh: tm: 8 (over z, core), space: 4 (over y, x).
Axes of the slice: x: 2, y: 2, z: 4, core: 2. Of those that a mesh axis runs over, the one named last changes fastest.
Arguments:
- solution: float32 [512, 384, 384], P('tm', 'space'), may hold values from -6 to 6
- residual: float32 [512, 384, 384], P('tm', 'space'), may hold values from -6 to 6
- direction: float32 [512, 384, 384], P('tm', 'space'), may hold values from -6 to 6
- reaction: float32 [512, 384, 384], P('tm', 'space'), may hold values from 0.1 to 2
- time_bands: float32 [2, 4, 512], replicated, may hold values from -0.25 to 1.1, as said below
- space_bands: float32 [2, 4, 384], replicated, may hold values from -0.25 to 1.1, as said below
- time_basis: float32 [512, 512], replicated, may hold values from -0.25 to 0.25
- space_basis: float32 [384, 384], replicated, may hold values from -0.3125 to 0.3125
- time_eigen: float32 [512], replicated, may hold values from 0.1 to 1
- space_eigen: float32 [384], replicated, may hold values from 0.1 to 1
Outputs:
- new_solution: float32 [512, 384, 384], P('tm', 'space')
- new_residual: float32 [512, 384, 384], P('tm', 'space')
- new_direction: float32 [512, 384, 384], P('tm', 'space')
Inputs may be any that keep to these rules, and one draw needn't show every extreme that they name: `time_bands`: each of the two matrices is symmetric with every diagonal entry larger than the sum of the magnitudes of the other entries of its row. `space_bands`: each of the two matrices is symmetric with every diagonal entry larger than the sum of the magnitudes of the other entries of its row.
All inputs are finite; a program needn't handle non-finite values.
Results may differ from a plain program's by a relative error of at most 0.000051.
Values sent between devices are 32-bit elements; how exact they have to be, the bound alone decides.
No kernel may reach another device: no remote copies, remote signals or barrier semaphores. Data moves between devices by JAX's collectives and lax.ppermute only.
A program may use at most 192 MiB of HBM per device.

v0:
```python
import functools

import jax
import jax.numpy as jnp
from jax import lax
from jax.experimental import pallas as pl
from jax.experimental.pallas import tpu as pltpu
from jax.sharding import PartitionSpec as P


LANES = 128
f32 = jnp.float32
bf16 = jnp.bfloat16


def cost(flops, nbytes):
    return pl.CostEstimate(flops=int(flops), bytes_accessed=int(nbytes), transcendentals=0)


def params(mib):
    return pltpu.CompilerParams(
        dimension_semantics=("arbitrary",), vmem_limit_bytes=mib * 1024 * 1024
    )


def ordered_call(body, after, in_specs, mib=40, **rest):
    def gated(*refs):
        return body(*refs[len(after) :])

    call = pl.pallas_call(
        gated,
        in_specs=[pl.BlockSpec(memory_space=pl.ANY)] * len(after) + list(in_specs),
        compiler_params=params(mib),
        **rest,
    )
    return lambda *args: call(*after, *args)


def halves(value):
    high = value.astype(bf16)
    return high, (value - high.astype(f32)).astype(bf16)


def halves_outside(value):
    high = lax.reduce_precision(value, 8, 7)
    return high.astype(bf16), (value - high).astype(bf16)


def dot(left, right):
    return jnp.dot(left, right, preferred_element_type=f32)


def dot_rows(left, right):
    return lax.dot_general(left, right, (((1,), (1,)), ((), ())), preferred_element_type=f32)


def dot3(left, right):
    return dot(left[0], right[0]) + (dot(left[0], right[1]) + dot(left[1], right[0]))


def swap_slots(arrays):
    count = len(arrays)
    width = LANES // count
    slot = lax.broadcasted_iota(jnp.int32, arrays[0].shape, 1) // width
    arrays = list(arrays)
    bit = 1
    while bit < count:
        upper = (slot & bit) != 0
        for i in range(count):
            if i & bit:
                continue
            low, high = arrays[i], arrays[i | bit]
            arrays[i] = jnp.where(upper, pltpu.roll(high, bit * width, 1), low)
            arrays[i | bit] = jnp.where(upper, high, pltpu.roll(low, LANES - bit * width, 1))
        bit *= 2
    return arrays


def y_forward_body(group, field_ref, weight_ref, *rest):
    outs, held = rest[:-1], rest[-1]
    rows, _, depth = field_ref.shape
    high, low = halves(field_ref[...].reshape(rows * group, depth))
    both = dot_rows(jnp.concatenate([high, low], axis=1), weight_ref[...])
    held[...] = both[:, :LANES] + both[:, LANES:]
    blocks = swap_slots([held[pl.ds(i, rows, stride=group), :] for i in range(group)])
    for out, block in zip(outs, blocks):
        out[0] = block


def y_forward(field, weight, group, mib, after=()):
    rows, columns, depth = field.shape
    count = columns // group
    return ordered_call(
        functools.partial(y_forward_body, group),
        after,
        mib=mib,
        grid=(count,),
        in_specs=[
            pl.BlockSpec((rows, group, depth), lambda g: (0, g, 0)),
            pl.BlockSpec((2 * LANES, 2 * depth), lambda g: (0, 0)),
        ],
        out_specs=[pl.BlockSpec((1, rows, LANES), lambda g: (g, 0, 0))] * group,
        out_shape=[jax.ShapeDtypeStruct((count, rows, LANES), f32)] * group,
        scratch_shapes=[pltpu.VMEM((rows * group, LANES), f32)],
        cost_estimate=cost(
            6 * rows * columns * depth * LANES, 4 * rows * columns * (depth + LANES)
        ),
        name="y_forward",
    )(field, weight)


def partner_rows(me, k, size):
    return pl.ds(pl.multiple_of((me ^ k) * size, 8), size)


def t_forward_body(group, per_step, shares, place_ref, *refs):
    parts, high_ref, low_ref, outs = (
        refs[:group],
        refs[group],
        refs[group + 1],
        refs[group + 2 : -1],
    )
    held = refs[-1]
    rows, owned = held.shape[0] // group, held.shape[0] // shares
    for i in range(per_step):
        lanes = slice(i * LANES, (i + 1) * LANES)
        for e, part in enumerate(parts):
            held[partner_rows(place_ref[0], e, rows), lanes] = part[i]
    held[...] = dot3((high_ref[...], low_ref[...]), halves(held[...]))
    for i in range(per_step):
        lanes = slice(i * LANES, (i + 1) * LANES)
        for f, out in enumerate(outs):
            block = held[partner_rows(place_ref[1], f, owned), lanes]
            out[:, i * group : (i + 1) * group, :] = block.reshape(owned // group, group, LANES)


def t_forward(place, parts, high, low, shares, after=()):
    group = len(parts)
    count, rows, _ = parts[0].shape
    total = high.shape[0]
    owned = total // shares
    per_step = 2 if count % 2 == 0 else 1
    return ordered_call(
        functools.partial(t_forward_body, group, per_step, shares),
        after,
        grid=(count // per_step,),
        in_specs=[pl.BlockSpec(memory_space=pltpu.SMEM)]
        + [pl.BlockSpec((per_step, rows, LANES), lambda g: (g, 0, 0))] * group
        + [pl.BlockSpec((total, total), lambda g: (0, 0))] * 2,
        out_specs=[pl.BlockSpec((owned // group, per_step * group, LANES), lambda g: (0, g, 0))]
        * shares,
        out_shape=[jax.ShapeDtypeStruct((owned // group, count * group, LANES), f32)] * shares,
        cost_estimate=cost(6 * total * total * count * LANES, 8 * total * count * LANES),
        scratch_shapes=[pltpu.VMEM((total, per_step * LANES), f32)],
        name="t_forward",
    )(place, *parts, high, low)


def t_inverse_body(group, per_step, shares, place_ref, *refs):
    parts, high_ref, low_ref, outs = (
        refs[:shares],
        refs[shares],
        refs[shares + 1],
        refs[shares + 2 : -1],
    )
    held = refs[-1]
    rows, owned = held.shape[0] // group, held.shape[0] // shares
    for i in range(per_step):
        lanes = slice(i * LANES, (i + 1) * LANES)
        for f, part in enumerate(parts):
            held[partner_rows(place_ref[1], f, owned), lanes] = part[
                :, i * group : (i + 1) * group, :
            ].reshape(owned, LANES)
    held[...] = dot3((high_ref[...], low_ref[...]), halves(held[...]))
    for i in range(per_step):
        lanes = slice(i * LANES, (i + 1) * LANES)
        for e, out in enumerate(outs):
            out[i] = held[partner_rows(place_ref[0], e, rows), lanes]


def t_inverse(place, parts, high, low, group, after=()):
    shares = len(parts)
    bundles, lines, _ = parts[0].shape
    count = lines // group
    total = high.shape[0]
    rows = total // group
    per_step = 2 if count % 2 == 0 else 1
    return ordered_call(
        functools.partial(t_inverse_body, group, per_step, shares),
        after,
        grid=(count // per_step,),
        in_specs=[pl.BlockSpec(memory_space=pltpu.SMEM)]
        + [pl.BlockSpec((bundles, per_step * group, LANES), lambda g: (0, g, 0))] * shares
        + [pl.BlockSpec((total, total), lambda g: (0, 0))] * 2,
        out_specs=[pl.BlockSpec((per_step, rows, LANES), lambda g: (g, 0, 0))] * group,
        out_shape=[jax.ShapeDtypeStruct((count, rows, LANES), f32)] * group,
        cost_estimate=cost(6 * total * total * count * LANES, 8 * total * count * LANES),
        scratch_shapes=[pltpu.VMEM((total, per_step * LANES), f32)],
        name="t_inverse",
    )(place, *parts, high, low)


def gathered(me, parts, held, group):
    lines = parts[0].shape[1]
    pieces = []
    for h in range(2):
        for f, part in enumerate(parts):
            held[partner_rows(me, f, lines), :] = part[h]
        spread = [
            held[pl.ds(i, held.shape[0] // group, stride=group), :] for i in range(group)
        ]
        pieces.append(jnp.concatenate(swap_slots(spread), axis=0))
    return jnp.concatenate(pieces, axis=1)


def folded(values):
    return values.reshape(values.shape[0] // 8, 8, values.shape[1]).sum(0)


def x_first_body(group, shares, place_ref, *refs):
    parts = refs[:shares]
    high_ref, low_ref, lane_ref, column_ref, hat_ref, sum_ref, held = refs[shares:]
    hat = dot3((high_ref[...], low_ref[...]), halves(gathered(place_ref[1], parts, held, group)))
    hat_ref[0] = hat
    eigen_sum = column_ref[...] + lane_ref[0]

    @pl.when(pl.program_id(0) == 0)
    def _():
        sum_ref[...] = jnp.zeros_like(sum_ref)

    sum_ref[...] += folded(hat * (hat / eigen_sum))


def x_first(place, parts, high, low, lane_eigen, column_eigen, group, after=()):
    shares = len(parts)
    bundles, lines, _ = parts[0].shape
    wide = high.shape[0]
    return ordered_call(
        functools.partial(x_first_body, group, shares),
        after,
        grid=(bundles // 2,),
        in_specs=[pl.BlockSpec(memory_space=pltpu.SMEM)]
        + [pl.BlockSpec((2, lines, LANES), lambda g: (g, 0, 0))] * shares
        + [pl.BlockSpec((wide, wide), lambda g: (0, 0))] * 2
        + [
            pl.BlockSpec((1, 1, 2 * LANES), lambda g: (g, 0, 0)),
            pl.BlockSpec((wide, 1), lambda g: (0, 0)),
        ],
        out_specs=[
            pl.BlockSpec((1, wide, 2 * LANES), lambda g: (g, 0, 0)),
            pl.BlockSpec((8, 2 * LANES), lambda g: (0, 0)),
        ],
        out_shape=[
            jax.ShapeDtypeStruct((bundles // 2, wide, 2 * LANES), f32),
            jax.ShapeDtypeStruct((8, 2 * LANES), f32),
        ],
        scratch_shapes=[pltpu.VMEM((shares * lines, LANES), f32)],
        cost_estimate=cost(
            6 * wide * wide * bundles * LANES, 8 * wide * bundles * LANES
        ),
        name="x_first",
    )(place, *parts, high, low, lane_eigen, column_eigen)


def x_second_body(group, shares, *refs):
    place_ref, step_ref, parts, refs = refs[0], refs[1], refs[2 : 2 + shares], refs[1:]
    (
        forward_high,
        forward_low,
        back_high,
        back_low,
        lane_ref,
        column_ref,
        hat_ref,
    ) = refs[1 + shares : 8 + shares]
    outs, sum_ref, held = refs[8 + shares : -2], refs[-2], refs[-1]
    image_hat = dot3((forward_high[...], forward_low[...]), halves(gathered(place_ref[1], parts, held, group)))
    new_hat = hat_ref[0] - step_ref[0] * image_hat
    spectral = new_hat / (column_ref[...] + lane_ref[0])

    @pl.when(pl.program_id(0) == 0)
    def _():
        sum_ref[...] = jnp.zeros_like(sum_ref)

    sum_ref[...] += folded(new_hat * spectral)
    back = dot3((back_high[...], back_low[...]), halves(spectral))
    lines = outs[0].shape[1]
    each = held.shape[0] // group
    for h in range(2):
        spread = swap_slots(
            [
                back[i * each : (i + 1) * each, h * LANES : (h + 1) * LANES]
                for i in range(group)
            ]
        )
        for i in range(group):
            held[pl.ds(i, each, stride=group), :] = spread[i]
        for f, out in enumerate(outs):
            out[h] = held[partner_rows(place_ref[1], f, lines), :]


def x_second(place, step, parts, forward, back, lane_eigen, column_eigen, hat, group, after=()):
    shares = len(parts)
    bundles, lines, _ = parts[0].shape
    wide = forward[0].shape[0]
    return ordered_call(
        functools.partial(x_second_body, group, shares),
        after,
        grid=(bundles // 2,),
        in_specs=[pl.BlockSpec(memory_space=pltpu.SMEM)] * 2
        + [pl.BlockSpec((2, lines, LANES), lambda g: (g, 0, 0))] * shares
        + [pl.BlockSpec((wide, wide), lambda g: (0, 0))] * 4
        + [
            pl.BlockSpec((1, 1, 2 * LANES), lambda g: (g, 0, 0)),
            pl.BlockSpec((wide, 1), lambda g: (0, 0)),
            pl.BlockSpec((1, wide, 2 * LANES), lambda g: (g, 0, 0)),
        ],
        out_specs=[pl.BlockSpec((2, lines, LANES), lambda g: (g, 0, 0))] * shares
        + [pl.BlockSpec((8, 2 * LANES), lambda g: (0, 0))],
        out_shape=[jax.ShapeDtypeStruct((bundles, lines, LANES), f32)] * shares
        + [jax.ShapeDtypeStruct((8, 2 * LANES), f32)],
        scratch_shapes=[pltpu.VMEM((shares * lines, LANES), f32)],
        cost_estimate=cost(
            12 * wide * wide * bundles * LANES, 12 * wide * bundles * LANES
        ),
        name="x_second",
    )(place, step, *parts, *forward, *back, lane_eigen, column_eigen, hat)


def y_inverse_body(group, chunks, scaled, *refs):
    scale_ref = refs[0]
    parts = refs[1 : 1 + chunks * group]
    high_ref, low_ref = refs[1 + chunks * group : 3 + chunks * group]
    bases, out, held = refs[3 + chunks * group : -2], refs[-2], refs[-1]
    rows = parts[0].shape[1]
    for k in range(chunks):
        spread = swap_slots([part[0] for part in parts[k * group : (k + 1) * group]])
        for i in range(group):
            held[k, pl.ds(i, rows, stride=group), :] = spread[i]
    high, low = halves(jnp.concatenate([held[k] for k in range(chunks)], axis=1))
    result = dot(high, low_ref[...]) + dot(
        jnp.concatenate([high, low], axis=1),
        jnp.concatenate([high_ref[...], high_ref[...]], axis=0),
    )
    result = result.reshape(out.shape)
    out[...] = result + (scale_ref[0] * bases[0][...] if scaled else bases[0][...])


def y_inverse(scale, parts, high, low, bases, group, scaled, after=()):
    chunks = len(parts) // group
    count, rows, _ = parts[0].shape
    depth = high.shape[1]
    block = pl.BlockSpec((rows, group, depth), lambda g: (0, g, 0))
    return ordered_call(
        functools.partial(y_inverse_body, group, chunks, scaled),
        after,
        mib=60,
        grid=(count,),
        in_specs=[pl.BlockSpec(memory_space=pltpu.SMEM)]
        + [pl.BlockSpec((1, rows, LANES), lambda g: (g, 0, 0))] * len(parts)
        + [pl.BlockSpec((chunks * LANES, depth), lambda g: (0, 0))] * 2
        + [block] * len(bases),
        out_specs=block,
        out_shape=jax.ShapeDtypeStruct((rows, count * group, depth), f32),
        scratch_shapes=[pltpu.VMEM((chunks, rows * group, LANES), f32)],
        cost_estimate=cost(
            6 * rows * count * group * depth * chunks * LANES,
            4 * rows * count * group * (depth * (1 + len(bases)) + chunks * LANES),
        ),
        name="y_inverse",
    )(scale, *parts, high, low, *bases)


def update_body(step_ref, solution_ref, residual_ref, direction_ref, image_ref, one_ref, two_ref):
    step = step_ref[0]
    one_ref[...] = solution_ref[...] + step * direction_ref[...]
    two_ref[...] = residual_ref[...] - step * image_ref[...]


def update(step, solution, residual, direction, image, after=()):
    rows, columns, depth = solution.shape
    block = pl.BlockSpec((2, columns, depth), lambda g: (g, 0, 0))
    return ordered_call(
        update_body,
        after,
        grid=(rows // 2,),
        in_specs=[pl.BlockSpec(memory_space=pltpu.SMEM)] + [block] * 4,
        out_specs=[block] * 2,
        out_shape=[jax.ShapeDtypeStruct(solution.shape, f32)] * 2,
        cost_estimate=cost(4 * rows * columns * depth, 24 * rows * columns * depth),
        name="update",
    )(step, solution, residual, direction, image)


STRIDE = 4
RING = 3 * STRIDE


def image_body(blocks, coefficient_ref, front_ref, back_ref, own_ref, edge_ref, *refs):
    y_refs, (x_ref, direction_ref, reaction_ref) = refs[:blocks], refs[blocks : blocks + 3]
    image_ref, sum_ref, planes, mass_ring, stiff_ring = refs[blocks + 3 :]
    step, last = pl.program_id(0), pl.num_programs(0) - 1
    _, columns, depth = own_ref.shape
    edges = edge_ref.shape[1]
    tall = columns + edges

    def take(source):
        for p in range(STRIDE):
            planes[p * tall : p * tall + columns, :] = source[p]

    pl.when(step == 0)(lambda: take(front_ref))
    pl.when(step == last)(lambda: take(back_ref))
    pl.when(jnp.logical_and(step > 0, step < last))(lambda: take(own_ref))
    for p in range(STRIDE):
        planes[p * tall + columns : (p + 1) * tall, :] = edge_ref[p]

    high, low = halves(planes[...])
    mass, stiff = [], []
    for c in range(blocks):
        near = slice(max(c - 1, 0) * LANES, min(c + 2, blocks) * LANES)
        both = dot(
            jnp.concatenate([high[:, near], low[:, near], high[:, near]], axis=1), y_refs[c][...]
        )
        mass.append(both[:, :LANES])
        stiff.append(both[:, LANES:])
    mass, stiff = jnp.concatenate(mass, axis=1), jnp.concatenate(stiff, axis=1)
    stacked = jnp.concatenate(
        [
            jnp.concatenate([part[p * tall : (p + 1) * tall] for part in (mass, stiff)], axis=0)
            for p in range(STRIDE)
        ],
        axis=1,
    )
    high, low = halves(stacked)
    wide = dot(x_ref[...], high)
    result = (wide[: 2 * columns] + wide[2 * columns :]) + dot(x_ref[: 2 * columns, :], low)
    slot = lax.rem(step, 3) * STRIDE
    for p in range(STRIDE):
        mass_ring[slot + p] = result[:columns, p * depth : (p + 1) * depth]
        stiff_ring[slot + p] = result[columns:, p * depth : (p + 1) * depth]

    @pl.when(step == 0)
    def _():
        sum_ref[...] = jnp.zeros_like(sum_ref)

    @pl.when(step >= 2)
    def _():
        for p in range(STRIDE):
            row = STRIDE * (step - 2) + p
            total = reaction_ref[p] * direction_ref[p]
            for o in range(7):
                place = lax.rem(row + o + STRIDE - 3, RING)
                total = total + (
                    coefficient_ref[row * 14 + o] * mass_ring[place]
                    + coefficient_ref[row * 14 + 7 + o] * stiff_ring[place]
                )
            image_ref[p] = total
            sum_ref[...] += folded(direction_ref[p] * total)


def neighbours(head, tail, axis):
    count = lax.axis_size(axis)
    even = lax.axis_index(axis) % 2 == 0
    received = []
    for first, sent in ((0, jnp.where(even, tail, head)), (1, jnp.where(even, head, tail))):
        pairs = [(i, i + 1) for i in range(first, count - 1, 2)]
        received.append(lax.ppermute(sent, axis, pairs + [(b, a) for a, b in pairs]))
    return jnp.where(even, received[1], received[0]), jnp.where(even, received[0], received[1])


def band_dense(row_bands, column_bands, row_at, column_at):
    distance = column_at[None, :] - row_at[:, None]
    total = jnp.zeros(distance.shape, f32)
    for k in range(4):
        total = jnp.where(distance == k, row_bands[k][:, None], total)
        if k:
            total = jnp.where(distance == -k, column_bands[k][None, :], total)
    return total


def apply_operator(direction, halos, reaction, time_bands, space_bands, after):
    rows, columns, depth = direction.shape
    blocks = depth // LANES
    plane = jnp.zeros((1, columns, depth), f32)
    before = jnp.concatenate([plane, halos[0]], axis=0)
    behind = jnp.concatenate([halos[1], plane], axis=0)

    def with_halos(part):
        return jnp.concatenate([part(halos[0]), part(direction), part(halos[1])], axis=0)

    edge = jnp.concatenate(
        neighbours(
            with_halos(lambda cells: cells[:, :3]),
            with_halos(lambda cells: cells[:, columns - 3 :]),
            "space",
        ),
        axis=1,
    )
    edge = jnp.pad(edge, ((1, 1), (0, 10), (0, 0)))
    whole = jnp.arange(depth)
    y_high, y_low = zip(
        *(
            halves_outside(band_dense(space_bands[m], space_bands[m], whole, whole))
            for m in (1, 0)
        )
    )
    y_parts = []
    for c in range(blocks):
        near = slice(max(c - 1, 0) * LANES, min(c + 2, blocks) * LANES)
        own = slice(c * LANES, (c + 1) * LANES)
        top, bottom = (
            jnp.concatenate([matrix[near, own] for matrix in matrices], axis=1)
            for matrices in (y_high, y_low)
        )
        y_parts.append(jnp.concatenate([top, top, bottom], axis=0))
    padded_space = jnp.pad(space_bands, ((0, 0), (0, 0), (3, 3)))
    near_x = lax.dynamic_slice_in_dim(
        padded_space, lax.axis_index("space") * columns, columns + 6, 2
    )
    row_at = jnp.arange(columns)
    column_at = jnp.concatenate(
        [row_at, jnp.arange(-3, 0), jnp.arange(columns, columns + 3), jnp.full((10,), -1000)]
    )
    x_columns = jnp.concatenate(
        [
            near_x[:, :, 3 : 3 + columns],
            near_x[:, :, :3],
            near_x[:, :, 3 + columns :],
            jnp.zeros((2, 4, 10), f32),
        ],
        axis=2,
    )
    x_stiff, x_mass = (
        band_dense(near_x[m, :, 3 : 3 + columns], x_columns[m], row_at, column_at)
        for m in (0, 1)
    )
    x_matrix = jnp.concatenate(
        [
            jnp.concatenate([x_mass, jnp.zeros_like(x_mass)], axis=1),
            jnp.concatenate([x_stiff, x_mass], axis=1),
        ],
        axis=0,
    )
    x_matrix = jnp.concatenate(halves_outside(x_matrix), axis=0)
    padded_time = jnp.pad(time_bands, ((0, 0), (0, 0), (3, 3)))
    near_t = lax.dynamic_slice_in_dim(padded_time, lax.axis_index("tm") * rows, rows + 6, 2)
    table = jnp.stack(
        [
            near_t[m, abs(o), 3 + min(o, 0) : 3 + min(o, 0) + rows]
            for m in (0, 1)
            for o in range(-3, 4)
        ],
        axis=1,
    ).reshape(-1)
    tall = columns + 16
    steps = rows // STRIDE + 2
    fixed = lambda array: pl.BlockSpec(array.shape, lambda g: (0,) * array.ndim)
    own = lambda late: pl.BlockSpec(
        (STRIDE, columns, depth), lambda g: (jnp.clip(g - late, 0, steps - 3), 0, 0)
    )
    return ordered_call(
        functools.partial(image_body, blocks),
        after,
        mib=56,
        grid=(steps,),
        in_specs=[pl.BlockSpec(memory_space=pltpu.SMEM), fixed(before), fixed(behind), own(1)]
        + [pl.BlockSpec((STRIDE, 16, depth), lambda g: (g, 0, 0))]
        + [fixed(part) for part in y_parts]
        + [fixed(x_matrix), own(2), own(2)],
        out_specs=[own(2), pl.BlockSpec((8, depth), lambda g: (0, 0))],
        out_shape=[
            jax.ShapeDtypeStruct((rows, columns, depth), f32),
            jax.ShapeDtypeStruct((8, depth), f32),
        ],
        scratch_shapes=[pltpu.VMEM((STRIDE * tall, depth), f32)]
        + [pltpu.VMEM((RING, columns, depth), f32)] * 2,
        cost_estimate=cost(
            12 * (rows + 6) * tall * depth * depth, 16 * rows * columns * depth
        ),
        name="image",
    )(table, before, behind, direction, edge, *y_parts, x_matrix, direction, reaction)


def exchange(blocks, axis):
    count = len(blocks)
    received = {
        k: lax.ppermute(blocks[k], axis, [(j, j ^ k) for j in range(count)])
        for k in range(count - 1, 0, -1)
    }
    return [blocks[0]] + [received[k] for k in range(1, count)]


def total_over(scalars):
    row = lax.broadcasted_iota(jnp.int32, (8, LANES), 0)
    packed = jnp.zeros((8, LANES), f32)
    for i, scalar in enumerate(scalars):
        packed = jnp.where(row == i, scalar, packed)
    for axis in ("space", "tm"):
        packed = sum(exchange([packed] * lax.axis_size(axis), axis))
    return [packed[i, 0] for i in range(len(scalars))]


def by_partner(values, axis, dim):
    count = lax.axis_size(axis)
    me = lax.axis_index(axis)
    return jnp.concatenate(
        [lax.dynamic_slice_in_dim(values, me ^ k, 1, dim) for k in range(count)], axis=dim
    )


def per_device(
    solution,
    residual,
    direction,
    reaction,
    time_bands,
    space_bands,
    time_basis,
    space_basis,
    time_eigen,
    space_eigen,
):
    rows, columns, depth = residual.shape
    group = lax.axis_size("tm")
    shares = lax.axis_size("space")
    me_t = lax.axis_index("tm")
    me_s = lax.axis_index("space")
    total = time_basis.shape[0]
    owned = total // shares
    width = LANES // group
    chunks = depth // LANES
    bundles = owned // group

    columns_first = by_partner(
        space_basis.T.reshape(chunks, group, width, depth), "tm", 1
    ).reshape(chunks, LANES, depth)
    y_high, y_low = halves_outside(columns_first)
    y_weights = jnp.concatenate([y_high, y_low], axis=1)
    y_weights = jnp.concatenate([y_weights, y_weights], axis=2)

    place = jnp.stack([me_t, me_s]).astype(jnp.int32)
    t_back = halves_outside(time_basis)
    t_ahead = halves_outside(time_basis.T)

    rows_first = (
        space_basis.reshape(shares, columns // group, group, depth)
        .transpose(2, 0, 1, 3)
        .reshape(shares * columns, depth)
    )
    x_back = halves_outside(rows_first)
    x_ahead = halves_outside(rows_first.T)

    own_time = lax.dynamic_slice_in_dim(time_eigen, me_s * owned, owned)
    own_space = lax.dynamic_slice_in_dim(
        space_eigen.reshape(chunks, group, width), me_t, 1, 1
    ).reshape(chunks, width)
    lane_eigen = (own_time[None, :, None] + own_space[:, None, :]).reshape(
        chunks, bundles // 2, 1, 2 * LANES
    )
    column_eigen = space_eigen[:, None]

    chain = []

    def kernel(call, *args):
        result = call(*args, chain[:])
        chain[:] = [result[0] if isinstance(result, (list, tuple)) else result]
        return result

    def y_ahead(field, k, name):
        blocks = kernel(y_forward, field, y_weights[k], group, 60 if name == "r" and k == 0 else 40)
        return exchange(blocks, "tm")

    def t_ahead_of(parts):
        blocks = kernel(t_forward, place, parts, *t_ahead, shares)
        return exchange(blocks, "space")

    def x_first_of(parts, k):
        return kernel(x_first, place, parts, *x_ahead, lane_eigen[k], column_eigen, group)

    def x_second_of(parts, k):
        *blocks, part = kernel(
            x_second,
            place,
            step,
            parts,
            x_ahead,
            x_back,
            lane_eigen[k],
            column_eigen,
            first[k][0],
            group,
        )
        return exchange(blocks, "space"), jnp.sum(part)

    def t_back_of(parts):
        blocks = kernel(t_inverse, place, parts, *t_back, group)
        return exchange(blocks, "tm")

    last = chunks - 1
    halos = neighbours(direction[:3], direction[rows - 3 :], "tm")
    sent = [y_ahead(residual, k, "r") for k in range(chunks)]
    image, curvature_parts = kernel(
        apply_operator, direction, halos, reaction, time_bands, space_bands
    )
    spread = [t_ahead_of(sent[0])]
    image_sent, first = [], []
    image_sent.append(y_ahead(image, 0, "i"))
    spread.append(t_ahead_of(sent[1]))
    first.append(x_first_of(spread[0], 0))
    for k in range(1, last):
        image_sent.append(y_ahead(image, k, "i"))
        spread.append(t_ahead_of(sent[k + 1]))
        first.append(x_first_of(spread[k], k))
    first.append(x_first_of(spread[last], last))
    norm_old, curvature = total_over(
        (sum(jnp.sum(part) for _, part in first), jnp.sum(curvature_parts))
    )
    step_size = norm_old / curvature
    step = step_size.reshape(1)
    image_spread = [t_ahead_of(image_sent[0])]
    image_sent.append(y_ahead(image, last, "i"))
    returned, back, sums = [], [], []
    for k in range(chunks):
        parts, part = x_second_of(image_spread[k], k)
        returned.append(parts)
        sums.append(part)
        if k < last:
            image_spread.append(t_ahead_of(image_sent[k + 1]))
            back.append(t_back_of(returned[k]))
    (norm_new,) = total_over((sum(sums),))
    back.append(t_back_of(returned[last]))
    scale = (norm_new / norm_old).reshape(1)
    new_solution, new_residual = kernel(update, step, solution, residual, direction, image)
    partial = kernel(
        y_inverse,
        scale,
        [part for parts in back[:last] for part in parts],
        y_high[:last].reshape(last * LANES, depth),
        y_low[:last].reshape(last * LANES, depth),
        (direction,),
        group,
        True,
    )
    new_direction = kernel(
        y_inverse, scale, back[last], y_high[last], y_low[last], (partial,), group, False
    )
    return (new_solution, new_residual, new_direction)


def solution(mesh):
    return jax.shard_map(
        per_device,
        mesh=mesh,
        in_specs=(
            P("tm", "space", None),
            P("tm", "space", None),
            P("tm", "space", None),
            P("tm", "space", None),
            P(),
            P(),
            P(),
            P(),
            P(),
            P(),
        ),
        out_specs=(P("tm", "space", None), P("tm", "space", None), P("tm", "space", None)),
        check_vma=False,
    )
```

profile of v0, /device:TPU:0, one launch (start us, length us, event | category | flops | bytes accessed | tf_op | source)
XLA Modules:
  0.0 1006.6 jit_solution(12651764988510373144)
XLA Ops:
  6.3 13.1 %y_forward.6 = (f32[12,64,128]{2,1,0:T(8,128)}, f32[12,64,128]{2,1,0:T(8,128)}, f32[12,64,128]{2,1,0:T(8,128)}, f32[12,64,128]{2,1,0:T(8,128)}, f32[12,64,128]{2...) custom-call(f32[64,96,384]{2,1,0:T(8,128)} %refs_3_.1, ...), custom_call_target="tpu_custom_call" | custom-call | flops 1811939328 | bytes 12582912 | tf_op jit(solution)/shard_map/y_forward/pallas_call | solution.py:36
  91.2 33.8 %collective-permute-done.7.refs_6_ = f32[12,64,128]{2,1,0:T(8,128)S(1)} collective-permute-done((f32[12,64,128]{2,1,0:T(8,128)S(1)}, f32[12,64,128]{2,1,0:T(8,128)S(1)}, u32[]{:S(2)}, u32[]{:S(2)}) %collective-permute-start.7) | collective-permute-done | bytes 393248 | tf_op jit(solution)/shard_map/ppermute | solution.py:587
  145.2 15.5 %collective-permute-start.15 = (f32[12,64,128]{2,1,0:T(8,128)}, f32[12,64,128]{2,1,0:T(8,128)}, u32[]{:S(2)}, u32[]{:S(2)}) collective-permute-start(f32[12,64,128]{2,1,0:T(8,128)} %get-tuple-element.141), channel_id=1, source_target_pairs={{0,20},{4,16},{8,28},{12,24},{16,4},{20,0},{24,12},{28,8},{1,21},{... | collective-permute-start | bytes 1179656 | tf_op jit(solution)/shard_map/ppermute | solution.py:587
  162.6 47.5 %image.1 = (f32[64,96,384]{2,1,0:T(8,128)}, f32[8,384]{1,0:T(8,128)}) custom-call(f32[12,64,128]{2,1,0:T(8,128)} %copy-done.47, f32[896]{0:T(1024)} %reshape.117.refs_1_, f32[4,96,384]{2,1,0:T(8,128)} %concatenate.72.refs_2_, f32[4,96,384]{2,1,0:T(8,128)} %concatenate.73.refs_3_, f32[64,96,384]{2,1,0:T(8,128)} %refs_20_.1, ...), custom_call_target="tpu_custom_call" | custom-call | flops 13872660480 | bytes 37748736 | tf_op jit(solution)/shard_map/image/pallas_call | solution.py:36
  282.6 27.3 %collective-permute-done.24.refs_6_ = f32[12,64,128]{2,1,0:T(8,128)} collective-permute-done((f32[12,64,128]{2,1,0:T(8,128)}, f32[12,64,128]{2,1,0:T(8,128)}, u32[]{:S(2)}, u32[]{:S(2)}) %collective-permute-start.24) | collective-permute-done | bytes 393248 | tf_op jit(solution)/shard_map/ppermute | solution.py:587
  318.2 12.7 %y_forward.10 = (f32[12,64,128]{2,1,0:T(8,128)S(1)}, f32[12,64,128]{2,1,0:T(8,128)}, f32[12,64,128]{2,1,0:T(8,128)}, f32[12,64,128]{2,1,0:T(8,128)}, f32[12,64,1...) custom-call(f32[8,384,256]{2,1,0:T(8,128)S(1)} %get-tuple-element.148.ref, ...), custom_call_target="tpu_custom_call" | custom-call | flops 1811939328 | bytes 12582912 | tf_op jit(solution)/shard_map/y_forward/pallas_call | solution.py:36
  398.1 15.3 %collective-permute-done.37.refs_6_ = f32[12,64,128]{2,1,0:T(8,128)} collective-permute-done((f32[12,64,128]{2,1,0:T(8,128)}, f32[12,64,128]{2,1,0:T(8,128)}, u32[]{:S(2)}, u32[]{:S(2)}) %collective-permute-start.37) | collective-permute-done | bytes 393248 | tf_op jit(solution)/shard_map/ppermute | solution.py:587
  438.3 15.7 %collective-permute-start.48 = (f32[8,128]{1,0:T(8,128)S(1)}, f32[8,128]{1,0:T(8,128)S(1)}, u32[]{:S(2)}, u32[]{:S(2)}) collective-permute-start(f32[8,128]{1,0:T(8,128)S(1)} %add_add_fusion.3), channel_id=1, source_target_pairs={{0,20},{4,16},{8,28},{12,24},{16,4},{20,0},{24,12},{28,8},{1,21},{... | collective-permute-start | bytes 12296 | tf_op jit(solution)/shard_map/ppermute | solution.py:587
  478.3 18.5 %x_second.3 = (f32[16,96,128]{2,1,0:T(8,128)S(1)}, f32[16,96,128]{2,1,0:T(8,128)S(1)}, f32[16,96,128]{2,1,0:T(8,128)S(1)}, f32[16,96,128]{2,1,0:T(8,128)S(1)}, f32[8,256]{1,0:T(8,128)S(1)}) custom-call(f32[12,64,128]{2,1,0:T(8,128)S(1)} %get-tuple-element.174.refs_0_.refs_2_, s32[2]{0:T(128)S(1)} %pad_add_fusion.1.refs_1_, f32[1]{0:T(128)} %bitcast.41.refs_2_.refs_1_, ...), custom_call_target="tpu_custom_call" | custom-call | flops 3623878656 | bytes 9437184 | tf_op jit(solution)/shard_map/x_second/pallas_call | solution.py:36
  507.9 39.8 %collective-permute-done.57.refs_6_ = f32[12,64,128]{2,1,0:T(8,128)S(1)} collective-permute-done((f32[12,64,128]{2,1,0:T(8,128)S(1)}, f32[12,64,128]{2,1,0:T(8,128)S(1)}, u32[]{:S(2)}, u32[]{:S(2)}) %collective-permute-start.57) | collective-permute-done | bytes 393248 | tf_op jit(solution)/shard_map/ppermute | solution.py:587
  563.9 21.1 %collective-permute-done.62.refs_4_ = f32[16,96,128]{2,1,0:T(8,128)S(1)} collective-permute-done((f32[16,96,128]{2,1,0:T(8,128)S(1)}, f32[16,96,128]{2,1,0:T(8,128)S(1)}, u32[]{:S(2)}, u32[]{:S(2)}) %collective-permute-start.62) | collective-permute-done | bytes 786464 | tf_op jit(solution)/shard_map/ppermute | solution.py:587
  596.6 18.8 %collective-permute-done.65.refs_5_ = f32[16,96,128]{2,1,0:T(8,128)S(1)} collective-permute-done((f32[16,96,128]{2,1,0:T(8,128)S(1)}, f32[16,96,128]{2,1,0:T(8,128)S(1)}, u32[]{:S(2)}, u32[]{:S(2)}) %collective-permute-start.65) | collective-permute-done | bytes 786464 | tf_op jit(solution)/shard_map/ppermute | solution.py:587
  615.5 18.5 %x_second.4 = (f32[16,96,128]{2,1,0:T(8,128)S(1)}, f32[16,96,128]{2,1,0:T(8,128)S(1)}, f32[16,96,128]{2,1,0:T(8,128)S(1)}, f32[16,96,128]{2,1,0:T(8,128)S(1)}, f32[8,256]{1,0:T(8,128)S(1)}) custom-call(f32[12,64,128]{2,1,0:T(8,128)S(1)} %get-tuple-element.194.refs_0_.refs_2_, s32[2]{0:T(128)S(1)} %pad_add_fusion.1.refs_1_, f32[1]{0:T(128)} %bitcast.41.refs_2_.refs_1_, ...), custom_call_target="tpu_custom_call" | custom-call | flops 3623878656 | bytes 9437184 | tf_op jit(solution)/shard_map/x_second/pallas_call | solution.py:36
  640.6 38.4 %collective-permute-done.70.refs_6_ = f32[12,64,128]{2,1,0:T(8,128)S(1)} collective-permute-done((f32[12,64,128]{2,1,0:T(8,128)S(1)}, f32[12,64,128]{2,1,0:T(8,128)S(1)}, u32[]{:S(2)}, u32[]{:S(2)}) %collective-permute-start.70) | collective-permute-done | bytes 393248 | tf_op jit(solution)/shard_map/ppermute | solution.py:587
  694.3 22.0 %collective-permute-done.75.refs_4_ = f32[16,96,128]{2,1,0:T(8,128)S(1)} collective-permute-done((f32[16,96,128]{2,1,0:T(8,128)S(1)}, f32[16,96,128]{2,1,0:T(8,128)S(1)}, u32[]{:S(2)}, u32[]{:S(2)}) %collective-permute-start.75) | collective-permute-done | bytes 786464 | tf_op jit(solution)/shard_map/ppermute | solution.py:587
  727.5 18.2 %collective-permute-done.78.refs_5_ = f32[16,96,128]{2,1,0:T(8,128)S(1)} collective-permute-done((f32[16,96,128]{2,1,0:T(8,128)S(1)}, f32[16,96,128]{2,1,0:T(8,128)S(1)}, u32[]{:S(2)}, u32[]{:S(2)}) %collective-permute-start.78) | collective-permute-done | bytes 786464 | tf_op jit(solution)/shard_map/ppermute | solution.py:587
  745.7 19.3 %x_second.5 = (f32[16,96,128]{2,1,0:T(8,128)S(1)}, f32[16,96,128]{2,1,0:T(8,128)}, f32[16,96,128]{2,1,0:T(8,128)}, f32[16,96,128]{2,1,0:T(8,128)S(1)}, f32[8,256]{1,0:T(8,128)S(1)}) custom-call(f32[12,64,128]{2,1,0:T(8,128)S(1)} %get-tuple-element.210.refs_0_.refs_10_, s32[2]{0:T(128)S(1)} %pad_add_fusion.1.refs_1_, f32[1]{0:T(128)} %bitcast.41.refs_2_.refs_1_, ...), custom_call_target="tpu_custom_call" | custom-call | flops 3623878656 | bytes 9437184 | tf_op jit(solution)/shard_map/x_second/pallas_call | solution.py:36
  787.7 15.2 %collective-permute-done.85 = f32[8,128]{1,0:T(8,128)S(1)} collective-permute-done((f32[8,128]{1,0:T(8,128)S(1)}, f32[8,128]{1,0:T(8,128)S(1)}, u32[]{:S(2)}, u32[]{:S(2)}) %collective-permute-start.85) | collective-permute-done | bytes 4128 | tf_op jit(solution)/shard_map/ppermute | solution.py:587
  827.4 15.7 %collective-permute-start.90 = (f32[8,128]{1,0:T(8,128)S(1)}, f32[8,128]{1,0:T(8,128)S(1)}, u32[]{:S(2)}, u32[]{:S(2)}) collective-permute-start(f32[8,128]{1,0:T(8,128)S(1)} %add_add_fusion.1), channel_id=1, source_target_pairs={{0,20},{4,16},{8,28},{12,24},{16,4},{20,0},{24,12},{28,8},{1,21},{... | collective-permute-start | bytes 12296 | tf_op jit(solution)/shard_map/ppermute | solution.py:587
  885.2 23.9 %collective-permute-done.104.refs_15_ = f32[12,64,128]{2,1,0:T(8,128)S(1)} collective-permute-done((f32[12,64,128]{2,1,0:T(8,128)S(1)}, f32[12,64,128]{2,1,0:T(8,128)S(1)}, u32[]{:S(2)}, u32[]{:S(2)}) %collective-permute-start.104) | collective-permute-done | bytes 393248 | tf_op jit(solution)/shard_map/ppermute | solution.py:587
  918.7 16.4 %collective-permute-start.111 = (f32[12,64,128]{2,1,0:T(8,128)S(1)}, f32[12,64,128]{2,1,0:T(8,128)S(1)}, u32[]{:S(2)}, u32[]{:S(2)}) collective-permute-start(f32[12,64,128]{2,1,0:T(8,128)S(1)} %get-tuple-element.242), channel_id=1, source_target_pairs={{0,20},{4,16},{8,28},{12,24},{16,4},{20,0},{24,12},{28,8},{1,21},{... | collective-permute-start | bytes 1179656 | tf_op jit(solution)/shard_map/ppermute | solution.py:587
  944.3 28.0 %update.1 = (f32[64,96,384]{2,1,0:T(8,128)}, f32[64,96,384]{2,1,0:T(8,128)}) custom-call(f32[12,64,128]{2,1,0:T(8,128)S(1)} %get-tuple-element.218.refs_0_.refs_2_, f32[1]{0:T(128)} %bitcast.41.refs_2_.refs_1_, f32[64,96,384]{2,1,0:T(8,128)S(1)} %copy-done.4, f32[64,96,384]{2,1,0:T(8,128)} %refs_3_.1, f32[64,96,384]{2,1,0:T(8,128)} %refs_20_.1, ...), custom_call_target="tpu_custom_call" | custom-call | flops 9437184 | bytes 56623104 | tf_op jit(solution)/shard_map/update/pallas_call | solution.py:36
  972.3 18.5 %y_inverse.2.refs_0_.refs_12_ = f32[64,96,384]{2,1,0:T(8,128)} custom-call(f32[64,96,384]{2,1,0:T(8,128)} %get-tuple-element.121.refs_0_, f32[1]{0:T(128)} %bitcast.42.refs_1_, f32[12,64,128]{2,1,0:T(8,128)} %copy-done.18, f32[12,64,128]{2,1,0:T(8,128)} %copy-done.123, f32[12,64,128]{2,1,0:T(8,128)} %copy-done.124, f32[12,64,128]{2,1,0:T(8,128)} %copy-done.125, ...), custom_call_target="tpu_custom_call" | custom-call | flops 3623878656 | bytes 25165824 | tf_op jit(solution)/shard_map/y_inverse/pallas_call | solution.py:36
  991.5 15.1 %y_inverse.3 = f32[64,96,384]{2,1,0:T(8,128)} custom-call(f32[64,96,384]{2,1,0:T(8,128)} %y_inverse.2.refs_0_.refs_12_, f32[1]{0:T(128)} %bitcast.42.refs_1_, f32[12,64,128]{2,1,0:T(8,128)} %copy-done.11, f32[12,64,128]{2,1,0:T(8,128)} %copy-done.132, f32[12,64,128]{2,1,0:T(8,128)} %copy-done.134, f32[12,64,128]{2,1,0:T(8,128)} %collective-permute-done.109.refs_5_, ...), custom_call_target="tpu_custom_call" | custom-call | flops 1811939328 | bytes 22020096 | tf_op jit(solution)/shard_map/y_inverse/pallas_call | solution.py:36
  (642 shorter events, 469.4 us)
Async XLA Ops:
  2.8 58.4 %collective-permute-start.1 = (f32[3,96,384]{2,1,0:T(8,128)}, f32[3,96,384]{2,1,0:T(8,128)S(1)}, u32[]{:S(2)}, u32[]{:S(2)}) collective-permute-start(f32[3,96,384]{2,1,0:T(8,128)} %get-tuple-element.255), channel_id=1, source_target_pairs={{0,4},{8,12},{16,20},{24,28},{4,0},{12,8},{20,16},{28,24},{1,5},{9... | collective-permute-start | bytes 1327112 | tf_op jit(solution)/shard_map/ppermute | solution.py:467
  3.3 57.9 %collective-permute-start = (f32[3,96,384]{2,1,0:T(8,128)}, f32[3,96,384]{2,1,0:T(8,128)}, u32[]{:S(2)}, u32[]{:S(2)}) collective-permute-start(f32[3,96,384]{2,1,0:T(8,128)} %get-tuple-element.256), channel_id=1, source_target_pairs={{4,8},{12,16},{20,24},{8,4},{16,12},{24,20},{5,9},{13,17},{21,25},... | collective-permute-start | bytes 1327112 | tf_op jit(solution)/shard_map/ppermute | solution.py:467
  19.4 59.0 %collective-permute-start.4 = (f32[12,64,128]{2,1,0:T(8,128)}, f32[12,64,128]{2,1,0:T(8,128)S(1)}, u32[]{:S(2)}, u32[]{:S(2)}) collective-permute-start(f32[12,64,128]{2,1,0:T(8,128)} %get-tuple-element.128), channel_id=1, source_target_pairs={{0,4},{4,0},{8,12},{12,8},{16,20},{20,16},{24,28},{28,24},{1,5},{5... | collective-permute-start | bytes 1179656 | tf_op jit(solution)/shard_map/ppermute | solution.py:587
  22.6 58.2 %collective-permute-start.5 = (f32[12,64,128]{2,1,0:T(8,128)}, f32[12,64,128]{2,1,0:T(8,128)S(1)}, u32[]{:S(2)}, u32[]{:S(2)}) collective-permute-start(f32[12,64,128]{2,1,0:T(8,128)} %get-tuple-element.129), channel_id=1, source_target_pairs={{0,8},{4,12},{8,0},{12,4},{16,24},{20,28},{24,16},{28,20},{1,9},{5... | collective-permute-start | bytes 1179656 | tf_op jit(solution)/shard_map/ppermute | solution.py:587
  24.2 56.7 %collective-permute-start.6 = (f32[12,64,128]{2,1,0:T(8,128)}, f32[12,64,128]{2,1,0:T(8,128)}, u32[]{:S(2)}, u32[]{:S(2)}) collective-permute-start(f32[12,64,128]{2,1,0:T(8,128)} %get-tuple-element.130), channel_id=1, source_target_pairs={{0,12},{4,8},{8,4},{12,0},{16,28},{20,24},{24,20},{28,16},{1,13},{... | collective-permute-start | bytes 1179656 | tf_op jit(solution)/shard_map/ppermute | solution.py:587
  83.3 61.1 %collective-permute-start.10 = (f32[12,64,128]{2,1,0:T(8,128)S(1)}, f32[12,64,128]{2,1,0:T(8,128)S(1)}, u32[]{:S(2)}, u32[]{:S(2)}) collective-permute-start(f32[12,64,128]{2,1,0:T(8,128)S(1)} %copy-done.156), channel_id=1, source_target_pairs={{0,28},{4,24},{8,20},{12,16},{16,12},{20,8},{24,4},{28,0},{1,29},{... | collective-permute-start | bytes 1179656 | tf_op jit(solution)/shard_map/ppermute | solution.py:587
  88.4 72.3 %collective-permute-start.11 = (f32[12,64,128]{2,1,0:T(8,128)S(1)}, f32[12,64,128]{2,1,0:T(8,128)S(1)}, u32[]{:S(2)}, u32[]{:S(2)}) collective-permute-start(f32[12,64,128]{2,1,0:T(8,128)S(1)} %copy-done.79), channel_id=1, source_target_pairs={{0,4},{4,0},{8,12},{12,8},{16,20},{20,16},{24,28},{28,24},{1,5},{5... | collective-permute-start | bytes 1179656 | tf_op jit(solution)/shard_map/ppermute | solution.py:587
  125.8 98.5 %collective-permute-start.12 = (f32[12,64,128]{2,1,0:T(8,128)}, f32[12,64,128]{2,1,0:T(8,128)}, u32[]{:S(2)}, u32[]{:S(2)}) collective-permute-start(f32[12,64,128]{2,1,0:T(8,128)} %get-tuple-element.138), channel_id=1, source_target_pairs={{0,8},{4,12},{8,0},{12,4},{16,24},{20,28},{24,16},{28,20},{1,9},{5... | collective-permute-start | bytes 1179656 | tf_op jit(solution)/shard_map/ppermute | solution.py:587
  132.3 92.6 %collective-permute-start.13 = (f32[12,64,128]{2,1,0:T(8,128)}, f32[12,64,128]{2,1,0:T(8,128)}, u32[]{:S(2)}, u32[]{:S(2)}) collective-permute-start(f32[12,64,128]{2,1,0:T(8,128)} %get-tuple-element.139), channel_id=1, source_target_pairs={{0,12},{4,8},{8,4},{12,0},{16,28},{20,24},{24,20},{28,16},{1,13},{... | collective-permute-start | bytes 1179656 | tf_op jit(solution)/shard_map/ppermute | solution.py:587
  133.1 94.0 %collective-permute-start.14 = (f32[12,64,128]{2,1,0:T(8,128)}, f32[12,64,128]{2,1,0:T(8,128)}, u32[]{:S(2)}, u32[]{:S(2)}) collective-permute-start(f32[12,64,128]{2,1,0:T(8,128)} %get-tuple-element.140), channel_id=1, source_target_pairs={{0,16},{4,20},{8,24},{12,28},{16,0},{20,4},{24,8},{28,12},{1,17},{... | collective-permute-start | bytes 1179656 | tf_op jit(solution)/shard_map/ppermute | solution.py:587
  145.2 82.1 %collective-permute-start.15 = (f32[12,64,128]{2,1,0:T(8,128)}, f32[12,64,128]{2,1,0:T(8,128)}, u32[]{:S(2)}, u32[]{:S(2)}) collective-permute-start(f32[12,64,128]{2,1,0:T(8,128)} %get-tuple-element.141), channel_id=1, source_target_pairs={{0,20},{4,16},{8,28},{12,24},{16,4},{20,0},{24,12},{28,8},{1,21},{... | collective-permute-start | bytes 1179656 | tf_op jit(solution)/shard_map/ppermute | solution.py:587
  161.4 67.7 %collective-permute-start.16 = (f32[12,64,128]{2,1,0:T(8,128)}, f32[12,64,128]{2,1,0:T(8,128)}, u32[]{:S(2)}, u32[]{:S(2)}) collective-permute-start(f32[12,64,128]{2,1,0:T(8,128)} %get-tuple-element.142), channel_id=1, source_target_pairs={{0,24},{4,28},{8,16},{12,20},{16,8},{20,12},{24,0},{28,4},{1,25},{... | collective-permute-start | bytes 1179656 | tf_op jit(solution)/shard_map/ppermute | solution.py:587
  266.7 67.3 %collective-permute-start.26 = (f32[12,64,128]{2,1,0:T(8,128)}, f32[12,64,128]{2,1,0:T(8,128)}, u32[]{:S(2)}, u32[]{:S(2)}) collective-permute-start(f32[12,64,128]{2,1,0:T(8,128)} %get-tuple-element.155), channel_id=1, source_target_pairs={{0,24},{4,28},{8,16},{12,20},{16,8},{20,12},{24,0},{28,4},{1,25},{... | collective-permute-start | bytes 1179656 | tf_op jit(solution)/shard_map/ppermute | solution.py:587
  268.8 65.1 %collective-permute-start.27 = (f32[12,64,128]{2,1,0:T(8,128)}, f32[12,64,128]{2,1,0:T(8,128)}, u32[]{:S(2)}, u32[]{:S(2)}) collective-permute-start(f32[12,64,128]{2,1,0:T(8,128)} %get-tuple-element.156), channel_id=1, source_target_pairs={{0,28},{4,24},{8,20},{12,16},{16,12},{20,8},{24,4},{28,0},{1,29},{... | collective-permute-start | bytes 1179656 | tf_op jit(solution)/shard_map/ppermute | solution.py:587
  270.2 72.9 %collective-permute-start.28 = (f32[16,96,128]{2,1,0:T(8,128)}, f32[16,96,128]{2,1,0:T(8,128)}, u32[]{:S(2)}, u32[]{:S(2)}) collective-permute-start(f32[16,96,128]{2,1,0:T(8,128)} %get-tuple-element.158), channel_id=1, source_target_pairs={{0,1},{1,0},{2,3},{3,2},{4,5},{5,4},{6,7},{7,6},{8,9},{9,8},{10,11... | collective-permute-start | bytes 2359304 | tf_op jit(solution)/shard_map/ppermute | solution.py:587
  496.9 65.4 %collective-permute-start.61 = (f32[16,96,128]{2,1,0:T(8,128)S(1)}, f32[16,96,128]{2,1,0:T(8,128)S(1)}, u32[]{:S(2)}, u32[]{:S(2)}) collective-permute-start(f32[16,96,128]{2,1,0:T(8,128)S(1)} %get-tuple-element.191), channel_id=1, source_target_pairs={{0,1},{1,0},{2,3},{3,2},{4,5},{5,4},{6,7},{7,6},{8,9},{9,8},{10,11... | collective-permute-start | bytes 2359304 | tf_op jit(solution)/shard_map/ppermute | solution.py:587
  634.0 58.7 %collective-permute-start.74 = (f32[16,96,128]{2,1,0:T(8,128)S(1)}, f32[16,96,128]{2,1,0:T(8,128)S(1)}, u32[]{:S(2)}, u32[]{:S(2)}) collective-permute-start(f32[16,96,128]{2,1,0:T(8,128)S(1)} %get-tuple-element.207), channel_id=1, source_target_pairs={{0,1},{1,0},{2,3},{3,2},{4,5},{5,4},{6,7},{7,6},{8,9},{9,8},{10,11... | collective-permute-start | bytes 2359304 | tf_op jit(solution)/shard_map/ppermute | solution.py:587
  766.0 87.5 %collective-permute-start.80 = (f32[16,96,128]{2,1,0:T(8,128)}, f32[16,96,128]{2,1,0:T(8,128)S(1)}, u32[]{:S(2)}, u32[]{:S(2)}) collective-permute-start(f32[16,96,128]{2,1,0:T(8,128)} %get-tuple-element.215), channel_id=1, source_target_pairs={{0,1},{1,0},{2,3},{3,2},{4,5},{5,4},{6,7},{7,6},{8,9},{9,8},{10,11... | collective-permute-start | bytes 2359304 | tf_op jit(solution)/shard_map/ppermute | solution.py:587
  767.6 85.9 %collective-permute-start.81 = (f32[16,96,128]{2,1,0:T(8,128)}, f32[16,96,128]{2,1,0:T(8,128)}, u32[]{:S(2)}, u32[]{:S(2)}) collective-permute-start(f32[16,96,128]{2,1,0:T(8,128)} %get-tuple-element.216), channel_id=1, source_target_pairs={{0,2},{1,3},{2,0},{3,1},{4,6},{5,7},{6,4},{7,5},{8,10},{9,11},{10,... | collective-permute-start | bytes 2359304 | tf_op jit(solution)/shard_map/ppermute | solution.py:587
  768.1 85.9 %collective-permute-start.82 = (f32[16,96,128]{2,1,0:T(8,128)S(1)}, f32[16,96,128]{2,1,0:T(8,128)}, u32[]{:S(2)}, u32[]{:S(2)}) collective-permute-start(f32[16,96,128]{2,1,0:T(8,128)S(1)} %get-tuple-element.217), channel_id=1, source_target_pairs={{0,3},{1,2},{2,1},{3,0},{4,7},{5,6},{6,5},{7,4},{8,11},{9,10},{10,... | collective-permute-start | bytes 2359304 | tf_op jit(solution)/shard_map/ppermute | solution.py:587
  909.1 81.6 %collective-permute-start.109 = (f32[12,64,128]{2,1,0:T(8,128)}, f32[12,64,128]{2,1,0:T(8,128)}, u32[]{:S(2)}, u32[]{:S(2)}) collective-permute-start(f32[12,64,128]{2,1,0:T(8,128)} %get-tuple-element.240), channel_id=1, source_target_pairs={{0,12},{4,8},{8,4},{12,0},{16,28},{20,24},{24,20},{28,16},{1,13},{... | collective-permute-start | bytes 1179656 | tf_op jit(solution)/shard_map/ppermute | solution.py:587
  909.1 81.6 %collective-permute-start.110 = (f32[12,64,128]{2,1,0:T(8,128)}, f32[12,64,128]{2,1,0:T(8,128)}, u32[]{:S(2)}, u32[]{:S(2)}) collective-permute-start(f32[12,64,128]{2,1,0:T(8,128)} %get-tuple-element.241), channel_id=1, source_target_pairs={{0,16},{4,20},{8,24},{12,28},{16,0},{20,4},{24,8},{28,12},{1,17},{... | collective-permute-start | bytes 1179656 | tf_op jit(solution)/shard_map/ppermute | solution.py:587
  918.7 72.0 %collective-permute-start.111 = (f32[12,64,128]{2,1,0:T(8,128)S(1)}, f32[12,64,128]{2,1,0:T(8,128)S(1)}, u32[]{:S(2)}, u32[]{:S(2)}) collective-permute-start(f32[12,64,128]{2,1,0:T(8,128)S(1)} %get-tuple-element.242), channel_id=1, source_target_pairs={{0,20},{4,16},{8,28},{12,24},{16,4},{20,0},{24,12},{28,8},{1,21},{... | collective-permute-start | bytes 1179656 | tf_op jit(solution)/shard_map/ppermute | solution.py:587
  935.1 55.7 %collective-permute-start.112 = (f32[12,64,128]{2,1,0:T(8,128)S(1)}, f32[12,64,128]{2,1,0:T(8,128)}, u32[]{:S(2)}, u32[]{:S(2)}) collective-permute-start(f32[12,64,128]{2,1,0:T(8,128)S(1)} %get-tuple-element.243), channel_id=1, source_target_pairs={{0,24},{4,28},{8,16},{12,20},{16,8},{20,12},{24,0},{28,4},{1,25},{... | collective-permute-start | bytes 1179656 | tf_op jit(solution)/shard_map/ppermute | solution.py:587
  (250 other events, 5445.5 us)
where the time goes:
time: 1010 us
  waiting for transfers between devices  363 us (36%)
  Pallas kernels  310 us (31%)
  starting transfers between devices  228 us (23%)
  local copies, waits for them, and re-layouts  76.1 us (8%)
  other arithmetic  20 us (2%)
    ppermute x110, waiting for transfers between devices, exchange(): lax.ppermute(blocks[k], axis, [(j, j ^ k) for j in range(count)])  359 us
    pallas_call x25, Pallas kernels, ordered_call(): return lambda *args: call(*after, *args)  310 us
    ppermute x110, starting transfers between devices, exchange(): lax.ppermute(blocks[k], axis, [(j, j ^ k) for j in range(count)])  221 us
    unnamed x330, local copies, waits for them, and re-layouts  58.7 us
  transfers between devices with their start and end apart: 114, of which 32 were waited for; matrix products, arithmetic and copies ran while one was open for 4% of the time, Pallas kernels for 29%

commit v1 on v0

--- a/solution.py
+++ b/solution.py
@@ -19,7 +19,7 @@
 
 def params(mib):
     return pltpu.CompilerParams(
-        dimension_semantics=("arbitrary",), vmem_limit_bytes=mib * 1024 * 1024
+        vmem_limit_bytes=mib * 1024 * 1024
     )
 
 
@@ -109,8 +109,9 @@
     )(field, weight)
 
 
-def partner_rows(me, k, size):
-    return pl.ds(pl.multiple_of((me ^ k) * size, 8), size)
+def partner_rows(me, k, size, piece=0, pieces=1):
+    share = size // pieces
+    return pl.ds(pl.multiple_of((me ^ k) * size + piece * share, 8), share)
 
 
 def t_forward_body(group, per_step, shares, place_ref, *refs):
@@ -129,16 +130,17 @@
     held[...] = dot3((high_ref[...], low_ref[...]), halves(held[...]))
     for i in range(per_step):
         lanes = slice(i * LANES, (i + 1) * LANES)
+        pieces = len(outs) // shares
         for f, out in enumerate(outs):
-            block = held[partner_rows(place_ref[1], f, owned), lanes]
-            out[:, i * group : (i + 1) * group, :] = block.reshape(owned // group, group, LANES)
-
-
-def t_forward(place, parts, high, low, shares, after=()):
+            block = held[partner_rows(place_ref[1], f % shares, owned, f // shares, pieces), lanes]
+            out[:, i * group : (i + 1) * group, :] = block.reshape(-1, group, LANES)
+
+
+def t_forward(place, parts, high, low, shares, pieces, after=()):
     group = len(parts)
     count, rows, _ = parts[0].shape
     total = high.shape[0]
-    owned = total // shares
+    bundles = total // shares // group // pieces
     per_step = 2 if count % 2 == 0 else 1
     return ordered_call(
         functools.partial(t_forward_body, group, per_step, shares),
@@ -147,30 +149,31 @@
         in_specs=[pl.BlockSpec(memory_space=pltpu.SMEM)]
         + [pl.BlockSpec((per_step, rows, LANES), lambda g: (g, 0, 0))] * group
         + [pl.BlockSpec((total, total), lambda g: (0, 0))] * 2,
-        out_specs=[pl.BlockSpec((owned // group, per_step * group, LANES), lambda g: (0, g, 0))]
-        * shares,
-        out_shape=[jax.ShapeDtypeStruct((owned // group, count * group, LANES), f32)] * shares,
+        out_specs=[pl.BlockSpec((bundles, per_step * group, LANES), lambda g: (0, g, 0))]
+        * (shares * pieces),
+        out_shape=[jax.ShapeDtypeStruct((bundles, count * group, LANES), f32)]
+        * (shares * pieces),
         cost_estimate=cost(6 * total * total * count * LANES, 8 * total * count * LANES),
         scratch_shapes=[pltpu.VMEM((total, per_step * LANES), f32)],
         name="t_forward",
     )(place, *parts, high, low)
 
 
-def t_inverse_body(group, per_step, shares, place_ref, *refs):
+def t_inverse_body(group, per_step, shares, halved, place_ref, *refs):
+    count = shares * halved
     parts, high_ref, low_ref, outs = (
-        refs[:shares],
-        refs[shares],
-        refs[shares + 1],
-        refs[shares + 2 : -1],
+        refs[:count],
+        refs[count],
+        refs[count + 1],
+        refs[count + 2 : -1],
     )
     held = refs[-1]
     rows, owned = held.shape[0] // group, held.shape[0] // shares
     for i in range(per_step):
         lanes = slice(i * LANES, (i + 1) * LANES)
         for f, part in enumerate(parts):
-            held[partner_rows(place_ref[1], f, owned), lanes] = part[
-                :, i * group : (i + 1) * group, :
-            ].reshape(owned, LANES)
+            rows_of = partner_rows(place_ref[1], f % shares, owned, f // shares, halved)
+            held[rows_of, lanes] = part[:, i * group : (i + 1) * group, :].reshape(-1, LANES)
     held[...] = dot3((high_ref[...], low_ref[...]), halves(held[...]))
     for i in range(per_step):
         lanes = slice(i * LANES, (i + 1) * LANES)
@@ -178,19 +181,23 @@
             out[i] = held[partner_rows(place_ref[0], e, rows), lanes]
 
 
-def t_inverse(place, parts, high, low, group, after=()):
-    shares = len(parts)
+def t_inverse(place, parts, high, low, group, piece, pieces, after=()):
+    shares = lax.axis_size("space")
+    halved = len(parts) // shares
     bundles, lines, _ = parts[0].shape
     count = lines // group
     total = high.shape[0]
     rows = total // group
     per_step = 2 if count % 2 == 0 else 1
+    steps = count // per_step
+    begin, end = (-(-steps * p // pieces) for p in (piece, piece + 1))
+    count = (end - begin) * per_step
     return ordered_call(
-        functools.partial(t_inverse_body, group, per_step, shares),
+        functools.partial(t_inverse_body, group, per_step, shares, halved),
         after,
-        grid=(count // per_step,),
+        grid=(end - begin,),
         in_specs=[pl.BlockSpec(memory_space=pltpu.SMEM)]
-        + [pl.BlockSpec((bundles, per_step * group, LANES), lambda g: (0, g, 0))] * shares
+        + [pl.BlockSpec((bundles, per_step * group, LANES), lambda g: (0, g + begin, 0))] * len(parts)
         + [pl.BlockSpec((total, total), lambda g: (0, 0))] * 2,
         out_specs=[pl.BlockSpec((per_step, rows, LANES), lambda g: (g, 0, 0))] * group,
         out_shape=[jax.ShapeDtypeStruct((count, rows, LANES), f32)] * group,
@@ -299,7 +306,7 @@
             out[h] = held[partner_rows(place_ref[1], f, lines), :]
 
 
-def x_second(place, step, parts, forward, back, lane_eigen, column_eigen, hat, group, after=()):
+def x_second(place, step, parts, forward, back, lane_eigen, column_eigen, hat, group, begin, after=()):
     shares = len(parts)
     bundles, lines, _ = parts[0].shape
     wide = forward[0].shape[0]
@@ -311,9 +318,9 @@
         + [pl.BlockSpec((2, lines, LANES), lambda g: (g, 0, 0))] * shares
         + [pl.BlockSpec((wide, wide), lambda g: (0, 0))] * 4
         + [
-            pl.BlockSpec((1, 1, 2 * LANES), lambda g: (g, 0, 0)),
+            pl.BlockSpec((1, 1, 2 * LANES), lambda g: (g + begin, 0, 0)),
             pl.BlockSpec((wide, 1), lambda g: (0, 0)),
-            pl.BlockSpec((1, wide, 2 * LANES), lambda g: (g, 0, 0)),
+            pl.BlockSpec((1, wide, 2 * LANES), lambda g: (g + begin, 0, 0)),
         ],
         out_specs=[pl.BlockSpec((2, lines, LANES), lambda g: (g, 0, 0))] * shares
         + [pl.BlockSpec((8, 2 * LANES), lambda g: (0, 0))],
@@ -331,7 +338,7 @@
     scale_ref = refs[0]
     parts = refs[1 : 1 + chunks * group]
     high_ref, low_ref = refs[1 + chunks * group : 3 + chunks * group]
-    bases, out, held = refs[3 + chunks * group : -2], refs[-2], refs[-1]
+    base_ref, out, held = refs[3 + chunks * group :]
     rows = parts[0].shape[1]
     for k in range(chunks):
         spread = swap_slots([part[0] for part in parts[k * group : (k + 1) * group]])
@@ -343,14 +350,14 @@
         jnp.concatenate([high_ref[...], high_ref[...]], axis=0),
     )
     result = result.reshape(out.shape)
-    out[...] = result + (scale_ref[0] * bases[0][...] if scaled else bases[0][...])
-
-
-def y_inverse(scale, parts, high, low, bases, group, scaled, after=()):
+    out[...] = result + (scale_ref[0] * base_ref[...] if scaled else base_ref[...])
+
+
+def y_inverse(scale, parts, high, low, base, group, scaled, begin=0, after=()):
     chunks = len(parts) // group
     count, rows, _ = parts[0].shape
     depth = high.shape[1]
-    block = pl.BlockSpec((rows, group, depth), lambda g: (0, g, 0))
+    block = pl.BlockSpec((rows, group, depth), lambda g: (0, g + begin, 0))
     return ordered_call(
         functools.partial(y_inverse_body, group, chunks, scaled),
         after,
@@ -359,16 +366,17 @@
         in_specs=[pl.BlockSpec(memory_space=pltpu.SMEM)]
         + [pl.BlockSpec((1, rows, LANES), lambda g: (g, 0, 0))] * len(parts)
         + [pl.BlockSpec((chunks * LANES, depth), lambda g: (0, 0))] * 2
-        + [block] * len(bases),
+        + [block],
         out_specs=block,
-        out_shape=jax.ShapeDtypeStruct((rows, count * group, depth), f32),
+        out_shape=jax.ShapeDtypeStruct(base.shape, f32),
         scratch_shapes=[pltpu.VMEM((chunks, rows * group, LANES), f32)],
+        input_output_aliases={} if scaled else {len(after) + len(parts) + 3: 0},
         cost_estimate=cost(
             6 * rows * count * group * depth * chunks * LANES,
-            4 * rows * count * group * (depth * (1 + len(bases)) + chunks * LANES),
+            4 * rows * count * group * (2 * depth + chunks * LANES),
         ),
         name="y_inverse",
-    )(scale, *parts, high, low, *bases)
+    )(scale, *parts, high, low, base)
 
 
 def update_body(step_ref, solution_ref, residual_ref, direction_ref, image_ref, one_ref, two_ref):
@@ -445,7 +453,8 @@
 
     @pl.when(step >= 2)
     def _():
-        for p in range(STRIDE):
+        @pl.loop(0, STRIDE)
+        def _(p):
             row = STRIDE * (step - 2) + p
             total = reaction_ref[p] * direction_ref[p]
             for o in range(7):
@@ -581,23 +590,46 @@
     )(table, before, behind, direction, edge, *y_parts, x_matrix, direction, reaction)
 
 
+def by_xor(block, axis, k):
+    return lax.ppermute(block, axis, [(j, j ^ k) for j in range(lax.axis_size(axis))])
+
+
 def exchange(blocks, axis):
     count = len(blocks)
-    received = {
-        k: lax.ppermute(blocks[k], axis, [(j, j ^ k) for j in range(count)])
-        for k in range(count - 1, 0, -1)
-    }
+    received = {k: by_xor(blocks[k], axis, k) for k in range(count - 1, 0, -1)}
     return [blocks[0]] + [received[k] for k in range(1, count)]
 
 
-def total_over(scalars):
+def gathered_totals(scalars):
     row = lax.broadcasted_iota(jnp.int32, (8, LANES), 0)
     packed = jnp.zeros((8, LANES), f32)
     for i, scalar in enumerate(scalars):
         packed = jnp.where(row == i, scalar, packed)
     for axis in ("space", "tm"):
-        packed = sum(exchange([packed] * lax.axis_size(axis), axis))
-    return [packed[i, 0] for i in range(len(scalars))]
+        packed = packed + by_xor(packed, axis, 1)
+        parts = [packed] + [by_xor(packed, axis, k) for k in range(lax.axis_size(axis) - 2, 0, -2)]
+        packed = sum(parts) if axis == "space" else packed
+    return parts
+
+
+def scale_body(old_ref, *refs):
+    total = refs[0][...]
+    for ref in refs[1:-1]:
+        total = total + ref[...]
+    refs[-1][...] = total / old_ref[0]
+
+
+def scale_kernel(old, parts, after=()):
+    return ordered_call(
+        scale_body,
+        after,
+        in_specs=[pl.BlockSpec(memory_space=pltpu.SMEM)]
+        + [pl.BlockSpec(memory_space=pltpu.VMEM)] * len(parts),
+        out_specs=pl.BlockSpec(memory_space=pltpu.VMEM),
+        out_shape=jax.ShapeDtypeStruct((8, LANES), f32),
+        cost_estimate=cost(8 * LANES * len(parts), 4096 * len(parts)),
+        name="scale",
+    )(old, *parts)
 
 
 def by_partner(values, axis, dim):
@@ -670,14 +702,16 @@
         blocks = kernel(y_forward, field, y_weights[k], group, 60 if name == "r" and k == 0 else 40)
         return exchange(blocks, "tm")
 
-    def t_ahead_of(parts):
-        blocks = kernel(t_forward, place, parts, *t_ahead, shares)
-        return exchange(blocks, "space")
+    def t_ahead_of(parts, pieces=1):
+        blocks = kernel(t_forward, place, parts, *t_ahead, shares, pieces)
+        if pieces == 1:
+            return exchange(blocks, "space")
+        return [exchange(blocks[p * shares : (p + 1) * shares], "space") for p in range(pieces)]
 
     def x_first_of(parts, k):
         return kernel(x_first, place, parts, *x_ahead, lane_eigen[k], column_eigen, group)
 
-    def x_second_of(parts, k):
+    def x_second_of(parts, k, piece=0, pieces=1):
         *blocks, part = kernel(
             x_second,
             place,
@@ -689,11 +723,12 @@
             column_eigen,
             first[k][0],
             group,
+            piece * (bundles // 2 // pieces),
         )
         return exchange(blocks, "space"), jnp.sum(part)
 
-    def t_back_of(parts):
-        blocks = kernel(t_inverse, place, parts, *t_back, group)
+    def t_back_of(parts, piece=0, pieces=1):
+        blocks = kernel(t_inverse, place, parts, *t_back, group, piece, pieces)
         return exchange(blocks, "tm")
 
     last = chunks - 1
@@ -703,46 +738,59 @@
         apply_operator, direction, halos, reaction, time_bands, space_bands
     )
     spread = [t_ahead_of(sent[0])]
-    image_sent, first = [], []
-    image_sent.append(y_ahead(image, 0, "i"))
-    spread.append(t_ahead_of(sent[1]))
-    first.append(x_first_of(spread[0], 0))
-    for k in range(1, last):
-        image_sent.append(y_ahead(image, k, "i"))
-        spread.append(t_ahead_of(sent[k + 1]))
-        first.append(x_first_of(spread[k], k))
+    image_sent, first = [y_ahead(image, 0, "i")], []
+    for k in range(1, chunks):
+        spread.append(t_ahead_of(sent[k]))
+        first.append(x_first_of(spread[k - 1], k - 1))
+        if k < last:
+            image_sent.append(y_ahead(image, k, "i"))
     first.append(x_first_of(spread[last], last))
-    norm_old, curvature = total_over(
-        (sum(jnp.sum(part) for _, part in first), jnp.sum(curvature_parts))
-    )
+    totals = sum(
+        gathered_totals((sum(jnp.sum(part) for _, part in first), jnp.sum(curvature_parts)))
+    )
+    norm_old, curvature = totals[0, 0], totals[1, 0]
     step_size = norm_old / curvature
     step = step_size.reshape(1)
     image_spread = [t_ahead_of(image_sent[0])]
-    image_sent.append(y_ahead(image, last, "i"))
+    image_sent += [y_ahead(image, k, "i") for k in range(len(image_sent), chunks)]
     returned, back, sums = [], [], []
-    for k in range(chunks):
+    pieces = 2 if bundles % 4 == 0 else 1
+    for k in range(last):
         parts, part = x_second_of(image_spread[k], k)
         returned.append(parts)
         sums.append(part)
-        if k < last:
-            image_spread.append(t_ahead_of(image_sent[k + 1]))
+        if k == 0 and last > 1:
+            image_spread.append(t_ahead_of(image_sent[1]))
+            back.append(t_back_of(returned[0]))
+        if k + 2 < last:
+            image_spread.append(t_ahead_of(image_sent[k + 2]))
+        if k == last - 1:
+            image_spread.append(t_ahead_of(image_sent[last], pieces))
+        if k >= len(back):
             back.append(t_back_of(returned[k]))
-    (norm_new,) = total_over((sum(sums),))
-    back.append(t_back_of(returned[last]))
-    scale = (norm_new / norm_old).reshape(1)
+    ready = image_spread[last] if pieces > 1 else [image_spread[last]]
+    returned_last = []
+    for piece, parts in enumerate(ready):
+        parts, part = x_second_of(parts, last, piece, pieces)
+        returned_last += parts
+        sums.append(part)
+    new_parts = gathered_totals((sum(sums),))
+    back_last = t_back_of(returned_last)
     new_solution, new_residual = kernel(update, step, solution, residual, direction, image)
+    scale = kernel(scale_kernel, norm_old.reshape(1), new_parts)[0, 0].reshape(1)
     partial = kernel(
         y_inverse,
         scale,
         [part for parts in back[:last] for part in parts],
         y_high[:last].reshape(last * LANES, depth),
         y_low[:last].reshape(last * LANES, depth),
-        (direction,),
+        direction,
         group,
         True,
-    )
-    new_direction = kernel(
-        y_inverse, scale, back[last], y_high[last], y_low[last], (partial,), group, False
+        0,
+    )
+    new_direction = y_inverse(
+        scale, back_last, y_high[last], y_low[last], partial, group, False
     )
     return (new_solution, new_residual, new_direction)
 

time: 1010 us -> 1030 us (1.020)
    unnamed x330 -> x332, local copies, waits for them, and re-layouts: 58.7 us -> 66.5 us
    ppermute x110 -> x108, starting transfers between devices: 221 us -> 226 us  [by_xor(): lax.ppermute(block, axis, [(j, j ^ k) for j in range(lax.axis_size(axis))])]
    pallas_call x25 -> x27, Pallas kernels: 310 us -> 312 us  [ordered_call(): return lambda *args: call(*after, *args)]
    ppermute x110 -> x108, waiting for transfers between devices: 359 us -> 361 us  [by_xor(): lax.ppermute(block, axis, [(j, j ^ k) for j in range(lax.axis_size(axis))])]
  transfers between devices with their start and end apart: 114 -> 112, of which waited for: 32 -> 31; matrix products, arithmetic and copies ran while one was open for 4% -> 4% of each run, Pallas kernels for 29% -> 28%
where the time goes in v1:
time: 1030 us; the launch traced here: 1020 us
  waiting for transfers between devices  364 us (35%)
  Pallas kernels  312 us (30%)
  starting transfers between devices  233 us (23%)
  local copies, waits for them, and re-layouts  83.9 us (8%)
  other arithmetic  21.5 us (2%)
    ppermute x108, waiting for transfers between devices, by_xor(): lax.ppermute(block, axis, [(j, j ^ k) for j in range(lax.axis_size(axis))])  361 us
    pallas_call x27, Pallas kernels, ordered_call(): return lambda *args: call(*after, *args)  312 us
    ppermute x108, starting transfers between devices, by_xor(): lax.ppermute(block, axis, [(j, j ^ k) for j in range(lax.axis_size(axis))])  226 us
    unnamed x332, local copies, waits for them, and re-layouts  66.5 us
  transfers between devices with their start and end apart: 112, of which 31 were waited for; matrix products, arithmetic and copies ran while one was open for 4% of the time, Pallas kernels for 28%

profile of v1, /device:TPU:0, one launch (start us, length us, event | category | flops | bytes accessed | tf_op | source)
XLA Modules:
  0.0 1022.0 jit_solution(3238939905988338274)
XLA Ops:
  6.3 13.1 %y_forward.6 = (f32[12,64,128]{2,1,0:T(8,128)}, f32[12,64,128]{2,1,0:T(8,128)}, f32[12,64,128]{2,1,0:T(8,128)}, f32[12,64,128]{2,1,0:T(8,128)}, f32[12,64,128]{2...) custom-call(f32[64,96,384]{2,1,0:T(8,128)} %refs_3_.1, ...), custom_call_target="tpu_custom_call" | custom-call | flops 1811939328 | bytes 12582912 | tf_op jit(solution)/shard_map/y_forward/pallas_call | solution.py:36
  91.1 33.9 %collective-permute-done.7.refs_6_ = f32[12,64,128]{2,1,0:T(8,128)S(1)} collective-permute-done((f32[12,64,128]{2,1,0:T(8,128)S(1)}, f32[12,64,128]{2,1,0:T(8,128)S(1)}, u32[]{:S(2)}, u32[]{:S(2)}) %collective-permute-start.7) | collective-permute-done | bytes 393248 | tf_op jit(solution)/shard_map/ppermute | solution.py:594
  145.1 15.5 %collective-permute-start.15 = (f32[12,64,128]{2,1,0:T(8,128)}, f32[12,64,128]{2,1,0:T(8,128)}, u32[]{:S(2)}, u32[]{:S(2)}) collective-permute-start(f32[12,64,128]{2,1,0:T(8,128)} %get-tuple-element.150), channel_id=1, source_target_pairs={{0,20},{4,16},{8,28},{12,24},{16,4},{20,0},{24,12},{28,8},{1,21},{... | collective-permute-start | bytes 1179656 | tf_op jit(solution)/shard_map/ppermute | solution.py:594
  162.6 44.1 %image.1 = (f32[64,96,384]{2,1,0:T(8,128)}, f32[8,384]{1,0:T(8,128)}) custom-call(f32[12,64,128]{2,1,0:T(8,128)} %copy-done.45, f32[896]{0:T(1024)} %reshape.112.refs_1_, f32[4,96,384]{2,1,0:T(8,128)} %concatenate.72.refs_2_, f32[4,96,384]{2,1,0:T(8,128)} %concatenate.73.refs_3_, f32[64,96,384]{2,1,0:T(8,128)} %refs_20_.1, ...), custom_call_target="tpu_custom_call" | custom-call | flops 13872660480 | bytes 37748736 | tf_op jit(solution)/shard_map/image/pallas_call | solution.py:36
  276.9 13.6 %y_forward.10 = (f32[12,64,128]{2,1,0:T(8,128)S(1)}, f32[12,64,128]{2,1,0:T(8,128)S(1)}, f32[12,64,128]{2,1,0:T(8,128)S(1)}, f32[12,64,128]{2,1,0:T(8,128)}, f32...) custom-call(f32[8,384,256]{2,1,0:T(8,128)S(1)} %get-tuple-element.157.refs_0_.ref, ...), custom_call_target="tpu_custom_call" | custom-call | flops 1811939328 | bytes 12582912 | tf_op jit(solution)/shard_map/y_forward/pallas_call | solution.py:36
  323.8 17.3 %collective-permute-done.29.refs_4_ = f32[16,96,128]{2,1,0:T(8,128)} collective-permute-done((f32[16,96,128]{2,1,0:T(8,128)}, f32[16,96,128]{2,1,0:T(8,128)}, u32[]{:S(2)}, u32[]{:S(2)}) %collective-permute-start.29) | collective-permute-done | bytes 786464 | tf_op jit(solution)/shard_map/ppermute | solution.py:594
  354.7 17.7 %collective-permute-done.32.refs_4_ = f32[16,96,128]{2,1,0:T(8,128)} collective-permute-done((f32[16,96,128]{2,1,0:T(8,128)}, f32[16,96,128]{2,1,0:T(8,128)}, u32[]{:S(2)}, u32[]{:S(2)}) %collective-permute-start.32) | collective-permute-done | bytes 786464 | tf_op jit(solution)/shard_map/ppermute | solution.py:594
  394.5 12.2 %collective-permute-done.36.refs_5_ = f32[12,64,128]{2,1,0:T(8,128)S(1)} collective-permute-done((f32[12,64,128]{2,1,0:T(8,128)}, f32[12,64,128]{2,1,0:T(8,128)S(1)}, u32[]{:S(2)}, u32[]{:S(2)}) %collective-permute-start.36) | collective-permute-done | bytes 393248 | tf_op jit(solution)/shard_map/ppermute | solution.py:594
  407.0 27.4 %collective-permute-done.37.refs_6_ = f32[12,64,128]{2,1,0:T(8,128)S(1)} collective-permute-done((f32[12,64,128]{2,1,0:T(8,128)}, f32[12,64,128]{2,1,0:T(8,128)S(1)}, u32[]{:S(2)}, u32[]{:S(2)}) %collective-permute-start.37) | collective-permute-done | bytes 393248 | tf_op jit(solution)/shard_map/ppermute | solution.py:594
  456.9 17.4 %collective-permute-start.46 = (f32[8,128]{1,0:T(8,128)S(1)}, f32[8,128]{1,0:T(8,128)S(1)}, u32[]{:S(2)}, u32[]{:S(2)}) collective-permute-start(f32[8,128]{1,0:T(8,128)S(1)} %add.139), channel_id=1, source_target_pairs={{0,8},{4,12},{8,0},{12,4},{16,24},{20,28},{24,16},{28,20},{1,9},{5... | collective-permute-start | bytes 12296 | tf_op jit(solution)/shard_map/ppermute | solution.py:594
  503.5 18.5 %x_second.4 = (f32[16,96,128]{2,1,0:T(8,128)S(1)}, f32[16,96,128]{2,1,0:T(8,128)S(1)}, f32[16,96,128]{2,1,0:T(8,128)S(1)}, f32[16,96,128]{2,1,0:T(8,128)S(1)}, f32[8,256]{1,0:T(8,128)S(1)}) custom-call(f32[12,64,128]{2,1,0:T(8,128)S(1)} %get-tuple-element.183.refs_0_.refs_2_, s32[2]{0:T(128)S(1)} %pad_add_fusion.1.refs_1_, f32[1]{0:T(128)} %bitcast.41.refs_2_.refs_1_, ...), custom_call_target="tpu_custom_call" | custom-call | flops 3623878656 | bytes 9437184 | tf_op jit(solution)/shard_map/x_second/pallas_call | solution.py:36
  522.1 29.2 %collective-permute-done.54.refs_7_ = f32[12,64,128]{2,1,0:T(8,128)S(1)} collective-permute-done((f32[12,64,128]{2,1,0:T(8,128)}, f32[12,64,128]{2,1,0:T(8,128)S(1)}, u32[]{:S(2)}, u32[]{:S(2)}) %collective-permute-start.54) | collective-permute-done | bytes 393248 | tf_op jit(solution)/shard_map/ppermute | solution.py:594
  557.2 16.5 %collective-permute-start.64 = (f32[12,64,128]{2,1,0:T(8,128)S(1)}, f32[12,64,128]{2,1,0:T(8,128)S(1)}, u32[]{:S(2)}, u32[]{:S(2)}) collective-permute-start(f32[12,64,128]{2,1,0:T(8,128)S(1)} %get-tuple-element.209), channel_id=1, source_target_pairs={{0,8},{4,12},{8,0},{12,4},{16,24},{20,28},{24,16},{28,20},{1,9},{5... | collective-permute-start | bytes 1179656 | tf_op jit(solution)/shard_map/ppermute | solution.py:594
  587.0 24.1 %collective-permute-done.61.refs_5_ = f32[16,96,128]{2,1,0:T(8,128)S(1)} collective-permute-done((f32[16,96,128]{2,1,0:T(8,128)S(1)}, f32[16,96,128]{2,1,0:T(8,128)S(1)}, u32[]{:S(2)}, u32[]{:S(2)}) %collective-permute-start.61) | collective-permute-done | bytes 786464 | tf_op jit(solution)/shard_map/ppermute | solution.py:594
  612.6 12.4 %collective-permute-start.67 = (f32[12,64,128]{2,1,0:T(8,128)}, f32[12,64,128]{2,1,0:T(8,128)S(1)}, u32[]{:S(2)}, u32[]{:S(2)}) collective-permute-start(f32[12,64,128]{2,1,0:T(8,128)} %get-tuple-element.212), channel_id=1, source_target_pairs={{0,20},{4,16},{8,28},{12,24},{16,4},{20,0},{24,12},{28,8},{1,21},{... | collective-permute-start | bytes 1179656 | tf_op jit(solution)/shard_map/ppermute | solution.py:594
  625.0 19.1 %collective-permute-done.58.refs_4_ = f32[16,96,128]{2,1,0:T(8,128)S(1)} collective-permute-done((f32[16,96,128]{2,1,0:T(8,128)S(1)}, f32[16,96,128]{2,1,0:T(8,128)S(1)}, u32[]{:S(2)}, u32[]{:S(2)}) %collective-permute-start.58) | collective-permute-done | bytes 786464 | tf_op jit(solution)/shard_map/ppermute | solution.py:594
  653.1 19.4 %x_second.5 = (f32[16,96,128]{2,1,0:T(8,128)S(1)}, f32[16,96,128]{2,1,0:T(8,128)}, f32[16,96,128]{2,1,0:T(8,128)}, f32[16,96,128]{2,1,0:T(8,128)}, f32[8,256]{1,0:T(8,128)S(1)}) custom-call(f32[12,64,128]{2,1,0:T(8,128)S(1)} %get-tuple-element.203.refs_0_.refs_2_, s32[2]{0:T(128)S(1)} %pad_add_fusion.1.refs_1_, f32[1]{0:T(128)} %bitcast.41.refs_2_.refs_1_, ...), custom_call_target="tpu_custom_call" | custom-call | flops 3623878656 | bytes 9437184 | tf_op jit(solution)/shard_map/x_second/pallas_call | solution.py:36
  688.0 30.1 %collective-permute-done.73.refs_4_ = f32[8,96,128]{2,1,0:T(8,128)S(1)} collective-permute-done((f32[8,96,128]{2,1,0:T(8,128)S(1)}, f32[8,96,128]{2,1,0:T(8,128)S(1)}, u32[]{:S(2)}, u32[]{:S(2)}) %collective-permute-start.73) | collective-permute-done | bytes 393248 | tf_op jit(solution)/shard_map/ppermute | solution.py:594
  786.1 30.2 %collective-permute-done.101.refs_6_ = f32[12,64,128]{2,1,0:T(8,128)} collective-permute-done((f32[12,64,128]{2,1,0:T(8,128)}, f32[12,64,128]{2,1,0:T(8,128)}, u32[]{:S(2)}, u32[]{:S(2)}) %collective-permute-start.101) | collective-permute-done | bytes 393248 | tf_op jit(solution)/shard_map/ppermute | solution.py:594
  886.3 31.7 %collective-permute-done.109.refs_15_ = f32[12,64,128]{2,1,0:T(8,128)S(1)} collective-permute-done((f32[12,64,128]{2,1,0:T(8,128)S(1)}, f32[12,64,128]{2,1,0:T(8,128)S(1)}, u32[]{:S(2)}, u32[]{:S(2)}) %collective-permute-start.109) | collective-permute-done | bytes 393248 | tf_op jit(solution)/shard_map/ppermute | solution.py:594
  927.1 16.6 %collective-permute-start.95 = (f32[12,64,128]{2,1,0:T(8,128)S(1)}, f32[12,64,128]{2,1,0:T(8,128)S(1)}, u32[]{:S(2)}, u32[]{:S(2)}) collective-permute-start(f32[12,64,128]{2,1,0:T(8,128)S(1)} %get-tuple-element.246), channel_id=1, source_target_pairs={{0,20},{4,16},{8,28},{12,24},{16,4},{20,0},{24,12},{28,8},{1,21},{... | collective-permute-start | bytes 1179656 | tf_op jit(solution)/shard_map/ppermute | solution.py:594
  953.1 28.0 %update.1 = (f32[64,96,384]{2,1,0:T(8,128)}, f32[64,96,384]{2,1,0:T(8,128)}) custom-call(f32[12,64,128]{2,1,0:T(8,128)S(1)} %get-tuple-element.235.refs_0_.refs_1_, f32[1]{0:T(128)} %bitcast.41.refs_2_.refs_1_, f32[64,96,384]{2,1,0:T(8,128)S(1)} %copy-done.4, f32[64,96,384]{2,1,0:T(8,128)} %refs_3_.1, f32[64,96,384]{2,1,0:T(8,128)} %refs_20_.1, ...), custom_call_target="tpu_custom_call" | custom-call | flops 9437184 | bytes 56623104 | tf_op jit(solution)/shard_map/update/pallas_call | solution.py:36
  985.9 19.0 %y_inverse.2.refs_11_ = f32[64,96,384]{2,1,0:T(8,128)} custom-call(f32[8,128]{1,0:T(8,128)} %copy-done.39, f32[1]{0:T(128)} %bitcast.43.refs_1_.refs_0_, f32[12,64,128]{2,1,0:T(8,128)} %copy-done.21, f32[12,64,128]{2,1,0:T(8,128)} %collective-permute-done.98.refs_3_, f32[12,64,128]{2,1,0:T(8,128)} %collective-permute-done.99.refs_4_, ...), custom_call_target="tpu_custom_call" | custom-call | flops 3623878656 | bytes 25165824 | tf_op jit(solution)/shard_map/y_inverse/pallas_call | solution.py:36
  1006.0 15.7 %y_inverse.3 = f32[64,96,384]{2,1,0:T(8,128)} custom-call(f32[1]{0:T(128)} %bitcast.43.refs_1_.refs_0_, f32[12,64,128]{2,1,0:T(8,128)} %copy-done.12, f32[12,64,128]{2,1,0:T(8,128)} %copy-done.131, f32[12,64,128]{2,1,0:T(8,128)} %copy-done.133, f32[12,64,128]{2,1,0:T(8,128)} %copy-done.135, ...), custom_call_target="tpu_custom_call", output_to_operand_aliasing={{}: (11, {})} | custom-call | flops 1811939328 | bytes 22020096 | tf_op jit(solution)/shard_map/y_inverse/pallas_call | solution.py:36
  (646 shorter events, 491.1 us)
Async XLA Ops:
  2.8 58.4 %collective-permute-start.1 = (f32[3,96,384]{2,1,0:T(8,128)}, f32[3,96,384]{2,1,0:T(8,128)S(1)}, u32[]{:S(2)}, u32[]{:S(2)}) collective-permute-start(f32[3,96,384]{2,1,0:T(8,128)} %get-tuple-element.273), channel_id=1, source_target_pairs={{0,4},{8,12},{16,20},{24,28},{4,0},{12,8},{20,16},{28,24},{1,5},{9... | collective-permute-start | bytes 1327112 | tf_op jit(solution)/shard_map/ppermute | solution.py:476
  3.3 57.9 %collective-permute-start = (f32[3,96,384]{2,1,0:T(8,128)}, f32[3,96,384]{2,1,0:T(8,128)}, u32[]{:S(2)}, u32[]{:S(2)}) collective-permute-start(f32[3,96,384]{2,1,0:T(8,128)} %get-tuple-element.274), channel_id=1, source_target_pairs={{4,8},{12,16},{20,24},{8,4},{16,12},{24,20},{5,9},{13,17},{21,25},... | collective-permute-start | bytes 1327112 | tf_op jit(solution)/shard_map/ppermute | solution.py:476
  19.4 59.0 %collective-permute-start.4 = (f32[12,64,128]{2,1,0:T(8,128)}, f32[12,64,128]{2,1,0:T(8,128)S(1)}, u32[]{:S(2)}, u32[]{:S(2)}) collective-permute-start(f32[12,64,128]{2,1,0:T(8,128)} %get-tuple-element.137), channel_id=1, source_target_pairs={{0,4},{4,0},{8,12},{12,8},{16,20},{20,16},{24,28},{28,24},{1,5},{5... | collective-permute-start | bytes 1179656 | tf_op jit(solution)/shard_map/ppermute | solution.py:594
  22.7 58.2 %collective-permute-start.5 = (f32[12,64,128]{2,1,0:T(8,128)}, f32[12,64,128]{2,1,0:T(8,128)S(1)}, u32[]{:S(2)}, u32[]{:S(2)}) collective-permute-start(f32[12,64,128]{2,1,0:T(8,128)} %get-tuple-element.138), channel_id=1, source_target_pairs={{0,8},{4,12},{8,0},{12,4},{16,24},{20,28},{24,16},{28,20},{1,9},{5... | collective-permute-start | bytes 1179656 | tf_op jit(solution)/shard_map/ppermute | solution.py:594
  83.3 61.1 %collective-permute-start.10 = (f32[12,64,128]{2,1,0:T(8,128)S(1)}, f32[12,64,128]{2,1,0:T(8,128)S(1)}, u32[]{:S(2)}, u32[]{:S(2)}) collective-permute-start(f32[12,64,128]{2,1,0:T(8,128)S(1)} %copy-done.157), channel_id=1, source_target_pairs={{0,28},{4,24},{8,20},{12,16},{16,12},{20,8},{24,4},{28,0},{1,29},{... | collective-permute-start | bytes 1179656 | tf_op jit(solution)/shard_map/ppermute | solution.py:594
  88.3 72.3 %collective-permute-start.11 = (f32[12,64,128]{2,1,0:T(8,128)S(1)}, f32[12,64,128]{2,1,0:T(8,128)S(1)}, u32[]{:S(2)}, u32[]{:S(2)}) collective-permute-start(f32[12,64,128]{2,1,0:T(8,128)S(1)} %copy-done.72), channel_id=1, source_target_pairs={{0,4},{4,0},{8,12},{12,8},{16,20},{20,16},{24,28},{28,24},{1,5},{5... | collective-permute-start | bytes 1179656 | tf_op jit(solution)/shard_map/ppermute | solution.py:594
  125.8 94.4 %collective-permute-start.12 = (f32[12,64,128]{2,1,0:T(8,128)}, f32[12,64,128]{2,1,0:T(8,128)}, u32[]{:S(2)}, u32[]{:S(2)}) collective-permute-start(f32[12,64,128]{2,1,0:T(8,128)} %get-tuple-element.147), channel_id=1, source_target_pairs={{0,8},{4,12},{8,0},{12,4},{16,24},{20,28},{24,16},{28,20},{1,9},{5... | collective-permute-start | bytes 1179656 | tf_op jit(solution)/shard_map/ppermute | solution.py:594
  132.3 88.5 %collective-permute-start.13 = (f32[12,64,128]{2,1,0:T(8,128)}, f32[12,64,128]{2,1,0:T(8,128)}, u32[]{:S(2)}, u32[]{:S(2)}) collective-permute-start(f32[12,64,128]{2,1,0:T(8,128)} %get-tuple-element.148), channel_id=1, source_target_pairs={{0,12},{4,8},{8,4},{12,0},{16,28},{20,24},{24,20},{28,16},{1,13},{... | collective-permute-start | bytes 1179656 | tf_op jit(solution)/shard_map/ppermute | solution.py:594
  133.1 89.9 %collective-permute-start.14 = (f32[12,64,128]{2,1,0:T(8,128)}, f32[12,64,128]{2,1,0:T(8,128)}, u32[]{:S(2)}, u32[]{:S(2)}) collective-permute-start(f32[12,64,128]{2,1,0:T(8,128)} %get-tuple-element.149), channel_id=1, source_target_pairs={{0,16},{4,20},{8,24},{12,28},{16,0},{20,4},{24,8},{28,12},{1,17},{... | collective-permute-start | bytes 1179656 | tf_op jit(solution)/shard_map/ppermute | solution.py:594
  145.1 78.0 %collective-permute-start.15 = (f32[12,64,128]{2,1,0:T(8,128)}, f32[12,64,128]{2,1,0:T(8,128)}, u32[]{:S(2)}, u32[]{:S(2)}) collective-permute-start(f32[12,64,128]{2,1,0:T(8,128)} %get-tuple-element.150), channel_id=1, source_target_pairs={{0,20},{4,16},{8,28},{12,24},{16,4},{20,0},{24,12},{28,8},{1,21},{... | collective-permute-start | bytes 1179656 | tf_op jit(solution)/shard_map/ppermute | solution.py:594
  161.4 63.6 %collective-permute-start.16 = (f32[12,64,128]{2,1,0:T(8,128)}, f32[12,64,128]{2,1,0:T(8,128)}, u32[]{:S(2)}, u32[]{:S(2)}) collective-permute-start(f32[12,64,128]{2,1,0:T(8,128)} %get-tuple-element.151), channel_id=1, source_target_pairs={{0,24},{4,28},{8,16},{12,20},{16,8},{20,12},{24,0},{28,4},{1,25},{... | collective-permute-start | bytes 1179656 | tf_op jit(solution)/shard_map/ppermute | solution.py:594
  263.7 57.2 %collective-permute-start.28 = (f32[16,96,128]{2,1,0:T(8,128)}, f32[16,96,128]{2,1,0:T(8,128)}, u32[]{:S(2)}, u32[]{:S(2)}) collective-permute-start(f32[16,96,128]{2,1,0:T(8,128)} %get-tuple-element.167), channel_id=1, source_target_pairs={{0,1},{1,0},{2,3},{3,2},{4,5},{5,4},{6,7},{7,6},{8,9},{9,8},{10,11... | collective-permute-start | bytes 2359304 | tf_op jit(solution)/shard_map/ppermute | solution.py:594
  583.6 60.5 %collective-permute-start.58 = (f32[16,96,128]{2,1,0:T(8,128)S(1)}, f32[16,96,128]{2,1,0:T(8,128)S(1)}, u32[]{:S(2)}, u32[]{:S(2)}) collective-permute-start(f32[16,96,128]{2,1,0:T(8,128)S(1)} %get-tuple-element.201), channel_id=1, source_target_pairs={{0,2},{1,3},{2,0},{3,1},{4,6},{5,7},{6,4},{7,5},{8,10},{9,11},{10,... | collective-permute-start | bytes 2359304 | tf_op jit(solution)/shard_map/ppermute | solution.py:594
  585.4 61.1 %collective-permute-start.59 = (f32[16,96,128]{2,1,0:T(8,128)S(1)}, f32[16,96,128]{2,1,0:T(8,128)S(1)}, u32[]{:S(2)}, u32[]{:S(2)}) collective-permute-start(f32[16,96,128]{2,1,0:T(8,128)S(1)} %get-tuple-element.202), channel_id=1, source_target_pairs={{0,3},{1,2},{2,1},{3,0},{4,7},{5,6},{6,5},{7,4},{8,11},{9,10},{10,... | collective-permute-start | bytes 2359304 | tf_op jit(solution)/shard_map/ppermute | solution.py:594
  611.1 61.4 %collective-permute-start.65 = (f32[12,64,128]{2,1,0:T(8,128)}, f32[12,64,128]{2,1,0:T(8,128)S(1)}, u32[]{:S(2)}, u32[]{:S(2)}) collective-permute-start(f32[12,64,128]{2,1,0:T(8,128)} %get-tuple-element.210), channel_id=1, source_target_pairs={{0,12},{4,8},{8,4},{12,0},{16,28},{20,24},{24,20},{28,16},{1,13},{... | collective-permute-start | bytes 1179656 | tf_op jit(solution)/shard_map/ppermute | solution.py:594
  611.1 63.2 %collective-permute-start.66 = (f32[12,64,128]{2,1,0:T(8,128)}, f32[12,64,128]{2,1,0:T(8,128)S(1)}, u32[]{:S(2)}, u32[]{:S(2)}) collective-permute-start(f32[12,64,128]{2,1,0:T(8,128)} %get-tuple-element.211), channel_id=1, source_target_pairs={{0,16},{4,20},{8,24},{12,28},{16,0},{20,4},{24,8},{28,12},{1,17},{... | collective-permute-start | bytes 1179656 | tf_op jit(solution)/shard_map/ppermute | solution.py:594
  612.6 62.0 %collective-permute-start.67 = (f32[12,64,128]{2,1,0:T(8,128)}, f32[12,64,128]{2,1,0:T(8,128)S(1)}, u32[]{:S(2)}, u32[]{:S(2)}) collective-permute-start(f32[12,64,128]{2,1,0:T(8,128)} %get-tuple-element.212), channel_id=1, source_target_pairs={{0,20},{4,16},{8,28},{12,24},{16,4},{20,0},{24,12},{28,8},{1,21},{... | collective-permute-start | bytes 1179656 | tf_op jit(solution)/shard_map/ppermute | solution.py:594
  886.2 57.5 %collective-permute-start.91 = (f32[12,64,128]{2,1,0:T(8,128)S(1)}, f32[12,64,128]{2,1,0:T(8,128)S(1)}, u32[]{:S(2)}, u32[]{:S(2)}) collective-permute-start(f32[12,64,128]{2,1,0:T(8,128)S(1)} %get-tuple-element.242), channel_id=1, source_target_pairs={{0,4},{4,0},{8,12},{12,8},{16,20},{20,16},{24,28},{28,24},{1,5},{5... | collective-permute-start | bytes 1179656 | tf_op jit(solution)/shard_map/ppermute | solution.py:594
  886.2 59.7 %collective-permute-start.92 = (f32[12,64,128]{2,1,0:T(8,128)S(1)}, f32[12,64,128]{2,1,0:T(8,128)S(1)}, u32[]{:S(2)}, u32[]{:S(2)}) collective-permute-start(f32[12,64,128]{2,1,0:T(8,128)S(1)} %get-tuple-element.243), channel_id=1, source_target_pairs={{0,8},{4,12},{8,0},{12,4},{16,24},{20,28},{24,16},{28,20},{1,9},{5... | collective-permute-start | bytes 1179656 | tf_op jit(solution)/shard_map/ppermute | solution.py:594
  918.1 86.9 %collective-permute-start.93 = (f32[12,64,128]{2,1,0:T(8,128)}, f32[12,64,128]{2,1,0:T(8,128)S(1)}, u32[]{:S(2)}, u32[]{:S(2)}) collective-permute-start(f32[12,64,128]{2,1,0:T(8,128)} %get-tuple-element.244), channel_id=1, source_target_pairs={{0,12},{4,8},{8,4},{12,0},{16,28},{20,24},{24,20},{28,16},{1,13},{... | collective-permute-start | bytes 1179656 | tf_op jit(solution)/shard_map/ppermute | solution.py:594
  918.1 86.9 %collective-permute-start.94 = (f32[12,64,128]{2,1,0:T(8,128)}, f32[12,64,128]{2,1,0:T(8,128)S(1)}, u32[]{:S(2)}, u32[]{:S(2)}) collective-permute-start(f32[12,64,128]{2,1,0:T(8,128)} %get-tuple-element.245), channel_id=1, source_target_pairs={{0,16},{4,20},{8,24},{12,28},{16,0},{20,4},{24,8},{28,12},{1,17},{... | collective-permute-start | bytes 1179656 | tf_op jit(solution)/shard_map/ppermute | solution.py:594
  927.1 77.9 %collective-permute-start.95 = (f32[12,64,128]{2,1,0:T(8,128)S(1)}, f32[12,64,128]{2,1,0:T(8,128)S(1)}, u32[]{:S(2)}, u32[]{:S(2)}) collective-permute-start(f32[12,64,128]{2,1,0:T(8,128)S(1)} %get-tuple-element.246), channel_id=1, source_target_pairs={{0,20},{4,16},{8,28},{12,24},{16,4},{20,0},{24,12},{28,8},{1,21},{... | collective-permute-start | bytes 1179656 | tf_op jit(solution)/shard_map/ppermute | solution.py:594
  943.7 61.4 %collective-permute-start.96 = (f32[12,64,128]{2,1,0:T(8,128)S(1)}, f32[12,64,128]{2,1,0:T(8,128)}, u32[]{:S(2)}, u32[]{:S(2)}) collective-permute-start(f32[12,64,128]{2,1,0:T(8,128)S(1)} %get-tuple-element.247), channel_id=1, source_target_pairs={{0,24},{4,28},{8,16},{12,20},{16,8},{20,12},{24,0},{28,4},{1,25},{... | collective-permute-start | bytes 1179656 | tf_op jit(solution)/shard_map/ppermute | solution.py:594
  946.0 59.1 %collective-permute-start.97 = (f32[12,64,128]{2,1,0:T(8,128)S(1)}, f32[12,64,128]{2,1,0:T(8,128)}, u32[]{:S(2)}, u32[]{:S(2)}) collective-permute-start(f32[12,64,128]{2,1,0:T(8,128)S(1)} %get-tuple-element.248), channel_id=1, source_target_pairs={{0,28},{4,24},{8,20},{12,16},{16,12},{20,8},{24,4},{28,0},{1,29},{... | collective-permute-start | bytes 1179656 | tf_op jit(solution)/shard_map/ppermute | solution.py:594
  (249 other events, 5368.8 us)

commit v2 on v1

--- a/solution.py
+++ b/solution.py
@@ -54,8 +54,12 @@
     return lax.dot_general(left, right, (((1,), (1,)), ((), ())), preferred_element_type=f32)
 
 
-def dot3(left, right):
-    return dot(left[0], right[0]) + (dot(left[0], right[1]) + dot(left[1], right[0]))
+def stacked_left(parts):
+    return jnp.concatenate([parts[0], parts[1], parts[0]], axis=1)
+
+
+def stacked_right(parts):
+    return jnp.concatenate([parts[0], parts[0], parts[1]], axis=0)
 
 
 def swap_slots(arrays):
@@ -115,19 +119,14 @@
 
 
 def t_forward_body(group, per_step, shares, place_ref, *refs):
-    parts, high_ref, low_ref, outs = (
-        refs[:group],
-        refs[group],
-        refs[group + 1],
-        refs[group + 2 : -1],
-    )
+    parts, weight_ref, outs = refs[:group], refs[group], refs[group + 1 : -1]
     held = refs[-1]
     rows, owned = held.shape[0] // group, held.shape[0] // shares
     for i in range(per_step):
         lanes = slice(i * LANES, (i + 1) * LANES)
         for e, part in enumerate(parts):
             held[partner_rows(place_ref[0], e, rows), lanes] = part[i]
-    held[...] = dot3((high_ref[...], low_ref[...]), halves(held[...]))
+    held[...] = dot(weight_ref[...], stacked_right(halves(held[...])))
     for i in range(per_step):
         lanes = slice(i * LANES, (i + 1) * LANES)
         pieces = len(outs) // shares
@@ -136,10 +135,10 @@
             out[:, i * group : (i + 1) * group, :] = block.reshape(-1, group, LANES)
 
 
-def t_forward(place, parts, high, low, shares, pieces, after=()):
+def t_forward(place, parts, weight, shares, pieces, after=()):
     group = len(parts)
     count, rows, _ = parts[0].shape
-    total = high.shape[0]
+    total = weight.shape[0]
     bundles = total // shares // group // pieces
     per_step = 2 if count % 2 == 0 else 1
     return ordered_call(
@@ -148,7 +147,7 @@
         grid=(count // per_step,),
         in_specs=[pl.BlockSpec(memory_space=pltpu.SMEM)]
         + [pl.BlockSpec((per_step, rows, LANES), lambda g: (g, 0, 0))] * group
-        + [pl.BlockSpec((total, total), lambda g: (0, 0))] * 2,
+        + [pl.BlockSpec((total, 3 * total), lambda g: (0, 0))],
         out_specs=[pl.BlockSpec((bundles, per_step * group, LANES), lambda g: (0, g, 0))]
         * (shares * pieces),
         out_shape=[jax.ShapeDtypeStruct((bundles, count * group, LANES), f32)]
@@ -156,17 +155,12 @@
         cost_estimate=cost(6 * total * total * count * LANES, 8 * total * count * LANES),
         scratch_shapes=[pltpu.VMEM((total, per_step * LANES), f32)],
         name="t_forward",
-    )(place, *parts, high, low)
+    )(place, *parts, weight)
 
 
 def t_inverse_body(group, per_step, shares, halved, place_ref, *refs):
     count = shares * halved
-    parts, high_ref, low_ref, outs = (
-        refs[:count],
-        refs[count],
-        refs[count + 1],
-        refs[count + 2 : -1],
-    )
+    parts, weight_ref, outs = refs[:count], refs[count], refs[count + 1 : -1]
     held = refs[-1]
     rows, owned = held.shape[0] // group, held.shape[0] // shares
     for i in range(per_step):
@@ -174,19 +168,19 @@
         for f, part in enumerate(parts):
             rows_of = partner_rows(place_ref[1], f % shares, owned, f // shares, halved)
             held[rows_of, lanes] = part[:, i * group : (i + 1) * group, :].reshape(-1, LANES)
-    held[...] = dot3((high_ref[...], low_ref[...]), halves(held[...]))
+    held[...] = dot(weight_ref[...], stacked_right(halves(held[...])))
     for i in range(per_step):
         lanes = slice(i * LANES, (i + 1) * LANES)
         for e, out in enumerate(outs):
             out[i] = held[partner_rows(place_ref[0], e, rows), lanes]
 
 
-def t_inverse(place, parts, high, low, group, piece, pieces, after=()):
+def t_inverse(place, parts, weight, group, piece, pieces, after=()):
     shares = lax.axis_size("space")
     halved = len(parts) // shares
     bundles, lines, _ = parts[0].shape
     count = lines // group
-    total = high.shape[0]
+    total = weight.shape[0]
     rows = total // group
     per_step = 2 if count % 2 == 0 else 1
     steps = count // per_step
@@ -198,13 +192,13 @@
         grid=(end - begin,),
         in_specs=[pl.BlockSpec(memory_space=pltpu.SMEM)]
         + [pl.BlockSpec((bundles, per_step * group, LANES), lambda g: (0, g + begin, 0))] * len(parts)
-        + [pl.BlockSpec((total, total), lambda g: (0, 0))] * 2,
+        + [pl.BlockSpec((total, 3 * total), lambda g: (0, 0))],
         out_specs=[pl.BlockSpec((per_step, rows, LANES), lambda g: (g, 0, 0))] * group,
         out_shape=[jax.ShapeDtypeStruct((count, rows, LANES), f32)] * group,
         cost_estimate=cost(6 * total * total * count * LANES, 8 * total * count * LANES),
         scratch_shapes=[pltpu.VMEM((total, per_step * LANES), f32)],
         name="t_inverse",
-    )(place, *parts, high, low)
+    )(place, *parts, weight)
 
 
 def gathered(me, parts, held, group):
@@ -226,8 +220,8 @@
 
 def x_first_body(group, shares, place_ref, *refs):
     parts = refs[:shares]
-    high_ref, low_ref, lane_ref, column_ref, hat_ref, sum_ref, held = refs[shares:]
-    hat = dot3((high_ref[...], low_ref[...]), halves(gathered(place_ref[1], parts, held, group)))
+    weight_ref, lane_ref, column_ref, hat_ref, sum_ref, held = refs[shares:]
+    hat = dot(weight_ref[...], stacked_right(halves(gathered(place_ref[1], parts, held, group))))
     hat_ref[0] = hat
     eigen_sum = column_ref[...] + lane_ref[0]
 
@@ -238,17 +232,17 @@
     sum_ref[...] += folded(hat * (hat / eigen_sum))
 
 
-def x_first(place, parts, high, low, lane_eigen, column_eigen, group, after=()):
+def x_first(place, parts, weight, lane_eigen, column_eigen, group, after=()):
     shares = len(parts)
     bundles, lines, _ = parts[0].shape
-    wide = high.shape[0]
+    wide = weight.shape[0]
     return ordered_call(
         functools.partial(x_first_body, group, shares),
         after,
         grid=(bundles // 2,),
         in_specs=[pl.BlockSpec(memory_space=pltpu.SMEM)]
         + [pl.BlockSpec((2, lines, LANES), lambda g: (g, 0, 0))] * shares
-        + [pl.BlockSpec((wide, wide), lambda g: (0, 0))] * 2
+        + [pl.BlockSpec((wide, 3 * wide), lambda g: (0, 0))]
         + [
             pl.BlockSpec((1, 1, 2 * LANES), lambda g: (g, 0, 0)),
             pl.BlockSpec((wide, 1), lambda g: (0, 0)),
@@ -266,22 +260,16 @@
             6 * wide * wide * bundles * LANES, 8 * wide * bundles * LANES
         ),
         name="x_first",
-    )(place, *parts, high, low, lane_eigen, column_eigen)
+    )(place, *parts, weight, lane_eigen, column_eigen)
 
 
 def x_second_body(group, shares, *refs):
     place_ref, step_ref, parts, refs = refs[0], refs[1], refs[2 : 2 + shares], refs[1:]
-    (
-        forward_high,
-        forward_low,
-        back_high,
-        back_low,
-        lane_ref,
-        column_ref,
-        hat_ref,
-    ) = refs[1 + shares : 8 + shares]
-    outs, sum_ref, held = refs[8 + shares : -2], refs[-2], refs[-1]
-    image_hat = dot3((forward_high[...], forward_low[...]), halves(gathered(place_ref[1], parts, held, group)))
+    forward_ref, back_ref, lane_ref, column_ref, hat_ref = refs[1 + shares : 6 + shares]
+    outs, sum_ref, held = refs[6 + shares : -2], refs[-2], refs[-1]
+    image_hat = dot(
+        forward_ref[...], stacked_right(halves(gathered(place_ref[1], parts, held, group)))
+    )
     new_hat = hat_ref[0] - step_ref[0] * image_hat
     spectral = new_hat / (column_ref[...] + lane_ref[0])
 
@@ -290,7 +278,7 @@
         sum_ref[...] = jnp.zeros_like(sum_ref)
 
     sum_ref[...] += folded(new_hat * spectral)
-    back = dot3((back_high[...], back_low[...]), halves(spectral))
+    back = dot(back_ref[...], stacked_right(halves(spectral)))
     lines = outs[0].shape[1]
     each = held.shape[0] // group
     for h in range(2):
@@ -309,14 +297,14 @@
 def x_second(place, step, parts, forward, back, lane_eigen, column_eigen, hat, group, begin, after=()):
     shares = len(parts)
     bundles, lines, _ = parts[0].shape
-    wide = forward[0].shape[0]
+    wide = forward.shape[0]
     return ordered_call(
         functools.partial(x_second_body, group, shares),
         after,
         grid=(bundles // 2,),
         in_specs=[pl.BlockSpec(memory_space=pltpu.SMEM)] * 2
         + [pl.BlockSpec((2, lines, LANES), lambda g: (g, 0, 0))] * shares
-        + [pl.BlockSpec((wide, wide), lambda g: (0, 0))] * 4
+        + [pl.BlockSpec((wide, 3 * wide), lambda g: (0, 0))] * 2
         + [
             pl.BlockSpec((1, 1, 2 * LANES), lambda g: (g + begin, 0, 0)),
             pl.BlockSpec((wide, 1), lambda g: (0, 0)),
@@ -331,32 +319,28 @@
             12 * wide * wide * bundles * LANES, 12 * wide * bundles * LANES
         ),
         name="x_second",
-    )(place, step, *parts, *forward, *back, lane_eigen, column_eigen, hat)
+    )(place, step, *parts, forward, back, lane_eigen, column_eigen, hat)
 
 
 def y_inverse_body(group, chunks, scaled, *refs):
     scale_ref = refs[0]
     parts = refs[1 : 1 + chunks * group]
-    high_ref, low_ref = refs[1 + chunks * group : 3 + chunks * group]
-    base_ref, out, held = refs[3 + chunks * group :]
+    weight_ref, base_ref, out, held = refs[1 + chunks * group :]
     rows = parts[0].shape[1]
     for k in range(chunks):
         spread = swap_slots([part[0] for part in parts[k * group : (k + 1) * group]])
         for i in range(group):
             held[k, pl.ds(i, rows, stride=group), :] = spread[i]
-    high, low = halves(jnp.concatenate([held[k] for k in range(chunks)], axis=1))
-    result = dot(high, low_ref[...]) + dot(
-        jnp.concatenate([high, low], axis=1),
-        jnp.concatenate([high_ref[...], high_ref[...]], axis=0),
-    )
+    data = jnp.concatenate([held[k] for k in range(chunks)], axis=1)
+    result = dot(stacked_left(halves(data)), weight_ref[...])
     result = result.reshape(out.shape)
     out[...] = result + (scale_ref[0] * base_ref[...] if scaled else base_ref[...])
 
 
-def y_inverse(scale, parts, high, low, base, group, scaled, begin=0, after=()):
+def y_inverse(scale, parts, weight, base, group, scaled, begin=0, after=()):
     chunks = len(parts) // group
     count, rows, _ = parts[0].shape
-    depth = high.shape[1]
+    depth = weight.shape[1]
     block = pl.BlockSpec((rows, group, depth), lambda g: (0, g + begin, 0))
     return ordered_call(
         functools.partial(y_inverse_body, group, chunks, scaled),
@@ -365,24 +349,27 @@
         grid=(count,),
         in_specs=[pl.BlockSpec(memory_space=pltpu.SMEM)]
         + [pl.BlockSpec((1, rows, LANES), lambda g: (g, 0, 0))] * len(parts)
-        + [pl.BlockSpec((chunks * LANES, depth), lambda g: (0, 0))] * 2
+        + [pl.BlockSpec((3 * chunks * LANES, depth), lambda g: (0, 0))]
         + [block],
         out_specs=block,
         out_shape=jax.ShapeDtypeStruct(base.shape, f32),
         scratch_shapes=[pltpu.VMEM((chunks, rows * group, LANES), f32)],
-        input_output_aliases={} if scaled else {len(after) + len(parts) + 3: 0},
+        input_output_aliases={} if scaled else {len(after) + len(parts) + 2: 0},
         cost_estimate=cost(
             6 * rows * count * group * depth * chunks * LANES,
             4 * rows * count * group * (2 * depth + chunks * LANES),
         ),
         name="y_inverse",
-    )(scale, *parts, high, low, base)
+    )(scale, *parts, weight, base)
 
 
 def update_body(step_ref, solution_ref, residual_ref, direction_ref, image_ref, one_ref, two_ref):
     step = step_ref[0]
-    one_ref[...] = solution_ref[...] + step * direction_ref[...]
-    two_ref[...] = residual_ref[...] - step * image_ref[...]
+
+    @pl.loop(0, one_ref.shape[0])
+    def _(p):
+        one_ref[p] = solution_ref[p] + step * direction_ref[p]
+        two_ref[p] = residual_ref[p] - step * image_ref[p]
 
 
 def update(step, solution, residual, direction, image, after=()):
@@ -413,8 +400,9 @@
     tall = columns + edges
 
     def take(source):
-        for p in range(STRIDE):
-            planes[p * tall : p * tall + columns, :] = source[p]
+        @pl.loop(0, STRIDE)
+        def _(p):
+            planes[pl.ds(pl.multiple_of(p * tall, 8), columns), :] = source[p]
 
     pl.when(step == 0)(lambda: take(front_ref))
     pl.when(step == last)(lambda: take(back_ref))
@@ -600,14 +588,17 @@
     return [blocks[0]] + [received[k] for k in range(1, count)]
 
 
-def gathered_totals(scalars):
+def gathered_totals(scalars, label):
     row = lax.broadcasted_iota(jnp.int32, (8, LANES), 0)
     packed = jnp.zeros((8, LANES), f32)
     for i, scalar in enumerate(scalars):
         packed = jnp.where(row == i, scalar, packed)
     for axis in ("space", "tm"):
-        packed = packed + by_xor(packed, axis, 1)
-        parts = [packed] + [by_xor(packed, axis, k) for k in range(lax.axis_size(axis) - 2, 0, -2)]
+        count = lax.axis_size(axis)
+        rounds = axis == "tm" or label == "total_a"
+        packed = packed + by_xor(packed, axis, 1) if rounds else packed
+        others = range(count - 2, 0, -2) if rounds else range(count - 1, 0, -1)
+        parts = [packed] + [by_xor(packed, axis, k) for k in others]
         packed = sum(parts) if axis == "space" else packed
     return parts
 
@@ -671,16 +662,16 @@
     y_weights = jnp.concatenate([y_weights, y_weights], axis=2)
 
     place = jnp.stack([me_t, me_s]).astype(jnp.int32)
-    t_back = halves_outside(time_basis)
-    t_ahead = halves_outside(time_basis.T)
+    t_back = stacked_left(halves_outside(time_basis))
+    t_ahead = stacked_left(halves_outside(time_basis.T))
 
     rows_first = (
         space_basis.reshape(shares, columns // group, group, depth)
         .transpose(2, 0, 1, 3)
         .reshape(shares * columns, depth)
     )
-    x_back = halves_outside(rows_first)
-    x_ahead = halves_outside(rows_first.T)
+    x_back = stacked_left(halves_outside(rows_first))
+    x_ahead = stacked_left(halves_outside(rows_first.T))
 
     own_time = lax.dynamic_slice_in_dim(time_eigen, me_s * owned, owned)
     own_space = lax.dynamic_slice_in_dim(
@@ -703,13 +694,13 @@
         return exchange(blocks, "tm")
 
     def t_ahead_of(parts, pieces=1):
-        blocks = kernel(t_forward, place, parts, *t_ahead, shares, pieces)
+        blocks = kernel(t_forward, place, parts, t_ahead, shares, pieces)
         if pieces == 1:
             return exchange(blocks, "space")
         return [exchange(blocks[p * shares : (p + 1) * shares], "space") for p in range(pieces)]
 
     def x_first_of(parts, k):
-        return kernel(x_first, place, parts, *x_ahead, lane_eigen[k], column_eigen, group)
+        return kernel(x_first, place, parts, x_ahead, lane_eigen[k], column_eigen, group)
 
     def x_second_of(parts, k, piece=0, pieces=1):
         *blocks, part = kernel(
@@ -728,7 +719,7 @@
         return exchange(blocks, "space"), jnp.sum(part)
 
     def t_back_of(parts, piece=0, pieces=1):
-        blocks = kernel(t_inverse, place, parts, *t_back, group, piece, pieces)
+        blocks = kernel(t_inverse, place, parts, t_back, group, piece, pieces)
         return exchange(blocks, "tm")
 
     last = chunks - 1
@@ -738,21 +729,20 @@
         apply_operator, direction, halos, reaction, time_bands, space_bands
     )
     spread = [t_ahead_of(sent[0])]
-    image_sent, first = [y_ahead(image, 0, "i")], []
+    image_sent, first = [y_ahead(image, k, "i") for k in range(chunks)], []
     for k in range(1, chunks):
         spread.append(t_ahead_of(sent[k]))
         first.append(x_first_of(spread[k - 1], k - 1))
-        if k < last:
-            image_sent.append(y_ahead(image, k, "i"))
     first.append(x_first_of(spread[last], last))
     totals = sum(
-        gathered_totals((sum(jnp.sum(part) for _, part in first), jnp.sum(curvature_parts)))
+        gathered_totals(
+            (sum(jnp.sum(part) for _, part in first), jnp.sum(curvature_parts)), "total_a"
+        )
     )
     norm_old, curvature = totals[0, 0], totals[1, 0]
     step_size = norm_old / curvature
     step = step_size.reshape(1)
     image_spread = [t_ahead_of(image_sent[0])]
-    image_sent += [y_ahead(image, k, "i") for k in range(len(image_sent), chunks)]
     returned, back, sums = [], [], []
     pieces = 2 if bundles % 4 == 0 else 1
     for k in range(last):
@@ -774,7 +764,7 @@
         parts, part = x_second_of(parts, last, piece, pieces)
         returned_last += parts
         sums.append(part)
-    new_parts = gathered_totals((sum(sums),))
+    new_parts = gathered_totals((sum(sums),), "total_b")
     back_last = t_back_of(returned_last)
     new_solution, new_residual = kernel(update, step, solution, residual, direction, image)
     scale = kernel(scale_kernel, norm_old.reshape(1), new_parts)[0, 0].reshape(1)
@@ -782,15 +772,14 @@
         y_inverse,
         scale,
         [part for parts in back[:last] for part in parts],
-        y_high[:last].reshape(last * LANES, depth),
-        y_low[:last].reshape(last * LANES, depth),
+        stacked_right([part[:last].reshape(last * LANES, depth) for part in (y_high, y_low)]),
         direction,
         group,
         True,
         0,
     )
     new_direction = y_inverse(
-        scale, back_last, y_high[last], y_low[last], partial, group, False
+        scale, back_last, stacked_right((y_high[last], y_low[last])), partial, group, False
     )
     return (new_solution, new_residual, new_direction)
 

time: 1030 us -> 1050 us (1.019)
  waiting for transfers between devices: 364 us -> 382 us
  Pallas kernels: 312 us -> 298 us
  starting transfers between devices: 233 us -> 244 us
    pallas_call x27, Pallas kernels: 312 us -> 298 us  [ordered_call(): return lambda *args: call(*after, *args)]
    ppermute x108 -> x109, starting transfers between devices: 226 us -> 237 us  [by_xor(): lax.ppermute(block, axis, [(j, j ^ k) for j in range(lax.axis_size(axis))])]
    ppermute x108 -> x109, waiting for transfers between devices: 361 us -> 369 us  [by_xor(): lax.ppermute(block, axis, [(j, j ^ k) for j in range(lax.axis_size(axis))])]
    unnamed x332 -> x384, local copies, waits for them, and re-layouts: 66.5 us -> 60.8 us
  transfers between devices with their start and end apart: 112 -> 113, of which waited for: 31 -> 31; matrix products, arithmetic and copies ran while one was open for 4% -> 5% of each run, Pallas kernels for 28% -> 27%
where the time goes in v2:
time: 1050 us; the launch traced here: 1040 us
  waiting for transfers between devices  382 us (36%)
  Pallas kernels  298 us (28%)
  starting transfers between devices  244 us (23%)
  local copies, waits for them, and re-layouts  77.8 us (7%)
  other arithmetic  30.9 us (3%)
    ppermute x109, waiting for transfers between devices, by_xor(): lax.ppermute(block, axis, [(j, j ^ k) for j in range(lax.axis_size(axis))])  369 us
    pallas_call x27, Pallas kernels, ordered_call(): return lambda *args: call(*after, *args)  298 us
    ppermute x109, starting transfers between devices, by_xor(): lax.ppermute(block, axis, [(j, j ^ k) for j in range(lax.axis_size(axis))])  237 us
    unnamed x384, local copies, waits for them, and re-layouts  60.8 us
  transfers between devices with their start and end apart: 113, of which 31 were waited for; matrix products, arithmetic and copies ran while one was open for 5% of the time, Pallas kernels for 27%

profile of v2, /device:TPU:0, one launch (start us, length us, event | category | flops | bytes accessed | tf_op | source)
XLA Modules:
  0.0 1041.0 jit_solution(18066962988342002254)
XLA Ops:
  6.3 13.4 %y_forward.6 = (f32[12,64,128]{2,1,0:T(8,128)}, f32[12,64,128]{2,1,0:T(8,128)}, f32[12,64,128]{2,1,0:T(8,128)}, f32[12,64,128]{2,1,0:T(8,128)}, f32[12,64,128]{2...) custom-call(f32[64,96,384]{2,1,0:T(8,128)} %refs_3_.1, ...), custom_call_target="tpu_custom_call" | custom-call | flops 1811939328 | bytes 12582912 | tf_op jit(solution)/shard_map/y_forward/pallas_call | solution.py:36
  104.1 22.4 %collective-permute-done.7.refs_6_ = f32[12,64,128]{2,1,0:T(8,128)S(1)} collective-permute-done((f32[12,64,128]{2,1,0:T(8,128)S(1)}, f32[12,64,128]{2,1,0:T(8,128)S(1)}, u32[]{:S(2)}, u32[]{:S(2)}) %collective-permute-start.7) | collective-permute-done | bytes 393248 | tf_op jit(solution)/shard_map/ppermute | solution.py:582
  133.8 44.4 %image.1 = (f32[64,96,384]{2,1,0:T(8,128)}, f32[8,384]{1,0:T(8,128)}) custom-call(f32[12,64,128]{2,1,0:T(8,128)} %copy-done.84, f32[896]{0:T(1024)} %reshape.112.refs_1_, f32[4,96,384]{2,1,0:T(8,128)} %concatenate.90.refs_2_, f32[4,96,384]{2,1,0:T(8,128)} %concatenate.91.refs_3_, f32[64,96,384]{2,1,0:T(8,128)} %refs_19_.1, ...), custom_call_target="tpu_custom_call" | custom-call | flops 13872660480 | bytes 37748736 | tf_op jit(solution)/shard_map/image/pallas_call | solution.py:36
  301.6 29.5 %collective-permute-done.24.refs_6_ = f32[12,64,128]{2,1,0:T(8,128)S(1)} collective-permute-done((f32[12,64,128]{2,1,0:T(8,128)}, f32[12,64,128]{2,1,0:T(8,128)S(1)}, u32[]{:S(2)}, u32[]{:S(2)}) %collective-permute-start.24) | collective-permute-done | bytes 393248 | tf_op jit(solution)/shard_map/ppermute | solution.py:582
  353.5 15.6 %collective-permute-done.29.refs_4_ = f32[16,96,128]{2,1,0:T(8,128)} collective-permute-done((f32[16,96,128]{2,1,0:T(8,128)}, f32[16,96,128]{2,1,0:T(8,128)}, u32[]{:S(2)}, u32[]{:S(2)}) %collective-permute-start.29) | collective-permute-done | bytes 786464 | tf_op jit(solution)/shard_map/ppermute | solution.py:582
  382.7 19.3 %collective-permute-done.32.refs_4_ = f32[16,96,128]{2,1,0:T(8,128)} collective-permute-done((f32[16,96,128]{2,1,0:T(8,128)}, f32[16,96,128]{2,1,0:T(8,128)}, u32[]{:S(2)}, u32[]{:S(2)}) %collective-permute-start.32) | collective-permute-done | bytes 786464 | tf_op jit(solution)/shard_map/ppermute | solution.py:582
  436.4 28.3 %collective-permute-done.37.refs_6_ = f32[12,64,128]{2,1,0:T(8,128)S(1)} collective-permute-done((f32[12,64,128]{2,1,0:T(8,128)}, f32[12,64,128]{2,1,0:T(8,128)S(1)}, u32[]{:S(2)}, u32[]{:S(2)}) %collective-permute-start.37) | collective-permute-done | bytes 393248 | tf_op jit(solution)/shard_map/ppermute | solution.py:582
  486.1 16.4 %collective-permute-start.46 = (f32[8,128]{1,0:T(8,128)S(1)}, f32[8,128]{1,0:T(8,128)S(1)}, u32[]{:S(2)}, u32[]{:S(2)}) collective-permute-start(f32[8,128]{1,0:T(8,128)S(1)} %add.142), channel_id=1, source_target_pairs={{0,8},{4,12},{8,0},{12,4},{16,24},{20,28},{24,16},{28,20},{1,9},{5... | collective-permute-start | bytes 12296 | tf_op jit(solution)/shard_map/ppermute | solution.py:582
  510.0 15.8 %collective-permute-done.51.refs_4_ = f32[12,64,128]{2,1,0:T(8,128)S(1)} collective-permute-done((f32[12,64,128]{2,1,0:T(8,128)S(1)}, f32[12,64,128]{2,1,0:T(8,128)S(1)}, u32[]{:S(2)}, u32[]{:S(2)}) %collective-permute-start.51) | collective-permute-done | bytes 393248 | tf_op jit(solution)/shard_map/ppermute | solution.py:582
  533.9 17.1 %x_second.4 = (f32[16,96,128]{2,1,0:T(8,128)S(1)}, f32[16,96,128]{2,1,0:T(8,128)S(1)}, f32[16,96,128]{2,1,0:T(8,128)S(1)}, f32[16,96,128]{2,1,0:T(8,128)S(1)}, f32[8,256]{1,0:T(8,128)S(1)}) custom-call(f32[16,96,128]{2,1,0:T(8,128)S(1)} %get-tuple-element.183.refs_0_.refs_3_, s32[2]{0:T(128)S(1)} %pad_add_fusion.1.refs_1_, f32[1]{0:T(128)} %bitcast.41.refs_2_.refs_1_, ...), custom_call_target="tpu_custom_call" | custom-call | flops 3623878656 | bytes 9437184 | tf_op jit(solution)/shard_map/x_second/pallas_call | solution.py:36
  551.0 19.1 %collective-permute-done.53.refs_6_ = f32[12,64,128]{2,1,0:T(8,128)S(1)} collective-permute-done((f32[12,64,128]{2,1,0:T(8,128)S(1)}, f32[12,64,128]{2,1,0:T(8,128)S(1)}, u32[]{:S(2)}, u32[]{:S(2)}) %collective-permute-start.53) | collective-permute-done | bytes 393248 | tf_op jit(solution)/shard_map/ppermute | solution.py:582
  583.9 13.1 %collective-permute-start.64 = (f32[12,64,128]{2,1,0:T(8,128)S(1)}, f32[12,64,128]{2,1,0:T(8,128)S(1)}, u32[]{:S(2)}, u32[]{:S(2)}) collective-permute-start(f32[12,64,128]{2,1,0:T(8,128)S(1)} %copy-done.69), channel_id=1, source_target_pairs={{0,8},{4,12},{8,0},{12,4},{16,24},{20,28},{24,16},{28,20},{1,9},{5... | collective-permute-start | bytes 1179656 | tf_op jit(solution)/shard_map/ppermute | solution.py:582
  609.6 25.2 %collective-permute-done.61.refs_5_ = f32[16,96,128]{2,1,0:T(8,128)S(1)} collective-permute-done((f32[16,96,128]{2,1,0:T(8,128)S(1)}, f32[16,96,128]{2,1,0:T(8,128)S(1)}, u32[]{:S(2)}, u32[]{:S(2)}) %collective-permute-start.61) | collective-permute-done | bytes 786464 | tf_op jit(solution)/shard_map/ppermute | solution.py:582
  635.8 14.2 %collective-permute-start.67 = (f32[12,64,128]{2,1,0:T(8,128)S(1)}, f32[12,64,128]{2,1,0:T(8,128)S(1)}, u32[]{:S(2)}, u32[]{:S(2)}) collective-permute-start(f32[12,64,128]{2,1,0:T(8,128)S(1)} %copy-done.63), channel_id=1, source_target_pairs={{0,20},{4,16},{8,28},{12,24},{16,4},{20,0},{24,12},{28,8},{1,21},{... | collective-permute-start | bytes 1179656 | tf_op jit(solution)/shard_map/ppermute | solution.py:582
  650.0 16.9 %collective-permute-done.58.refs_4_ = f32[16,96,128]{2,1,0:T(8,128)S(1)} collective-permute-done((f32[16,96,128]{2,1,0:T(8,128)S(1)}, f32[16,96,128]{2,1,0:T(8,128)S(1)}, u32[]{:S(2)}, u32[]{:S(2)}) %collective-permute-start.58) | collective-permute-done | bytes 786464 | tf_op jit(solution)/shard_map/ppermute | solution.py:582
  675.5 17.8 %x_second.5 = (f32[16,96,128]{2,1,0:T(8,128)S(1)}, f32[16,96,128]{2,1,0:T(8,128)}, f32[16,96,128]{2,1,0:T(8,128)}, f32[16,96,128]{2,1,0:T(8,128)}, f32[8,256]{1,0:T(8,128)S(1)}) custom-call(f32[12,64,128]{2,1,0:T(8,128)S(1)} %get-tuple-element.203.refs_0_.refs_2_, s32[2]{0:T(128)S(1)} %pad_add_fusion.1.refs_1_, f32[1]{0:T(128)} %bitcast.41.refs_2_.refs_1_, ...), custom_call_target="tpu_custom_call" | custom-call | flops 3623878656 | bytes 9437184 | tf_op jit(solution)/shard_map/x_second/pallas_call | solution.py:36
  708.5 30.0 %collective-permute-done.73.refs_4_ = f32[8,96,128]{2,1,0:T(8,128)S(1)} collective-permute-done((f32[8,96,128]{2,1,0:T(8,128)S(1)}, f32[8,96,128]{2,1,0:T(8,128)S(1)}, u32[]{:S(2)}, u32[]{:S(2)}) %collective-permute-start.73) | collective-permute-done | bytes 393248 | tf_op jit(solution)/shard_map/ppermute | solution.py:582
  800.0 36.4 %collective-permute-done.102.refs_6_ = f32[12,64,128]{2,1,0:T(8,128)} collective-permute-done((f32[12,64,128]{2,1,0:T(8,128)}, f32[12,64,128]{2,1,0:T(8,128)}, u32[]{:S(2)}, u32[]{:S(2)}) %collective-permute-start.102) | collective-permute-done | bytes 393248 | tf_op jit(solution)/shard_map/ppermute | solution.py:582
  848.3 13.4 %collective-permute-done.90.refs_4_ = f32[8,128]{1,0:T(8,128)S(1)} collective-permute-done((f32[8,128]{1,0:T(8,128)S(1)}, f32[8,128]{1,0:T(8,128)S(1)}, u32[]{:S(2)}, u32[]{:S(2)}) %collective-permute-start.90) | collective-permute-done | bytes 4128 | tf_op jit(solution)/shard_map/ppermute | solution.py:582
  909.2 28.9 %collective-permute-done.110.refs_15_ = f32[12,64,128]{2,1,0:T(8,128)S(1)} collective-permute-done((f32[12,64,128]{2,1,0:T(8,128)S(1)}, f32[12,64,128]{2,1,0:T(8,128)S(1)}, u32[]{:S(2)}, u32[]{:S(2)}) %collective-permute-start.110) | collective-permute-done | bytes 393248 | tf_op jit(solution)/shard_map/ppermute | solution.py:582
  949.6 16.3 %collective-permute-start.96 = (f32[12,64,128]{2,1,0:T(8,128)S(1)}, f32[12,64,128]{2,1,0:T(8,128)}, u32[]{:S(2)}, u32[]{:S(2)}) collective-permute-start(f32[12,64,128]{2,1,0:T(8,128)S(1)} %get-tuple-element.246), channel_id=1, source_target_pairs={{0,20},{4,16},{8,28},{12,24},{16,4},{20,0},{24,12},{28,8},{1,21},{... | collective-permute-start | bytes 1179656 | tf_op jit(solution)/shard_map/ppermute | solution.py:582
  972.8 28.0 %update.1 = (f32[64,96,384]{2,1,0:T(8,128)}, f32[64,96,384]{2,1,0:T(8,128)}) custom-call(f32[12,64,128]{2,1,0:T(8,128)S(1)} %get-tuple-element.235.refs_0_.refs_1_, f32[1]{0:T(128)} %bitcast.41.refs_2_.refs_1_, f32[64,96,384]{2,1,0:T(8,128)S(1)} %copy-done.5, f32[64,96,384]{2,1,0:T(8,128)} %refs_3_.1, f32[64,96,384]{2,1,0:T(8,128)} %refs_19_.1, ...), custom_call_target="tpu_custom_call" | custom-call | flops 9437184 | bytes 56623104 | tf_op jit(solution)/shard_map/update/pallas_call | solution.py:36
  1005.8 19.1 %y_inverse.2.refs_10_ = f32[64,96,384]{2,1,0:T(8,128)} custom-call(f32[8,128]{1,0:T(8,128)} %copy-done.47, f32[1]{0:T(128)} %bitcast.43.refs_1_.refs_0_, f32[12,64,128]{2,1,0:T(8,128)} %copy-done.46, f32[12,64,128]{2,1,0:T(8,128)} %collective-permute-done.99.refs_3_, f32[12,64,128]{2,1,0:T(8,128)} %collective-permute-done.100.refs_4_, ...), custom_call_target="tpu_custom_call" | custom-call | flops 3623878656 | bytes 25165824 | tf_op jit(solution)/shard_map/y_inverse/pallas_call | solution.py:36
  1024.9 15.8 %y_inverse.3 = f32[64,96,384]{2,1,0:T(8,128)} custom-call(f32[1]{0:T(128)} %bitcast.43.refs_1_.refs_0_, f32[12,64,128]{2,1,0:T(8,128)} %copy-done.17, f32[12,64,128]{2,1,0:T(8,128)} %copy-done.160, f32[12,64,128]{2,1,0:T(8,128)} %copy-done.162, f32[12,64,128]{2,1,0:T(8,128)} %collective-permute-done.94.refs_4_, ...), custom_call_target="tpu_custom_call", output_to_operand_aliasing={{}: (10, {})} | custom-call | flops 1811939328 | bytes 22020096 | tf_op jit(solution)/shard_map/y_inverse/pallas_call | solution.py:36
  (705 shorter events, 516.0 us)
Async XLA Ops:
  2.8 65.0 %collective-permute-start.1 = (f32[3,96,384]{2,1,0:T(8,128)}, f32[3,96,384]{2,1,0:T(8,128)}, u32[]{:S(2)}, u32[]{:S(2)}) collective-permute-start(f32[3,96,384]{2,1,0:T(8,128)} %get-tuple-element.273), channel_id=1, source_target_pairs={{0,4},{8,12},{16,20},{24,28},{4,0},{12,8},{20,16},{28,24},{1,5},{9... | collective-permute-start | bytes 1327112 | tf_op jit(solution)/shard_map/ppermute | solution.py:464
  3.3 64.5 %collective-permute-start = (f32[3,96,384]{2,1,0:T(8,128)}, f32[3,96,384]{2,1,0:T(8,128)}, u32[]{:S(2)}, u32[]{:S(2)}) collective-permute-start(f32[3,96,384]{2,1,0:T(8,128)} %get-tuple-element.274), channel_id=1, source_target_pairs={{4,8},{12,16},{20,24},{8,4},{16,12},{24,20},{5,9},{13,17},{21,25},... | collective-permute-start | bytes 1327112 | tf_op jit(solution)/shard_map/ppermute | solution.py:464
  19.7 80.3 %collective-permute-start.4 = (f32[12,64,128]{2,1,0:T(8,128)}, f32[12,64,128]{2,1,0:T(8,128)S(1)}, u32[]{:S(2)}, u32[]{:S(2)}) collective-permute-start(f32[12,64,128]{2,1,0:T(8,128)} %get-tuple-element.137), channel_id=1, source_target_pairs={{0,4},{4,0},{8,12},{12,8},{16,20},{20,16},{24,28},{28,24},{1,5},{5... | collective-permute-start | bytes 1179656 | tf_op jit(solution)/shard_map/ppermute | solution.py:582
  22.9 78.5 %collective-permute-start.5 = (f32[12,64,128]{2,1,0:T(8,128)}, f32[12,64,128]{2,1,0:T(8,128)}, u32[]{:S(2)}, u32[]{:S(2)}) collective-permute-start(f32[12,64,128]{2,1,0:T(8,128)} %get-tuple-element.138), channel_id=1, source_target_pairs={{0,8},{4,12},{8,0},{12,4},{16,24},{20,28},{24,16},{28,20},{1,9},{5... | collective-permute-start | bytes 1179656 | tf_op jit(solution)/shard_map/ppermute | solution.py:582
  24.5 79.4 %collective-permute-start.6 = (f32[12,64,128]{2,1,0:T(8,128)}, f32[12,64,128]{2,1,0:T(8,128)}, u32[]{:S(2)}, u32[]{:S(2)}) collective-permute-start(f32[12,64,128]{2,1,0:T(8,128)} %get-tuple-element.139), channel_id=1, source_target_pairs={{0,12},{4,8},{8,4},{12,0},{16,28},{20,24},{24,20},{28,16},{1,13},{... | collective-permute-start | bytes 1179656 | tf_op jit(solution)/shard_map/ppermute | solution.py:582
  100.0 78.2 %collective-permute-start.9 = (f32[12,64,128]{2,1,0:T(8,128)S(1)}, f32[12,64,128]{2,1,0:T(8,128)S(1)}, u32[]{:S(2)}, u32[]{:S(2)}) collective-permute-start(f32[12,64,128]{2,1,0:T(8,128)S(1)} %copy-done.184), channel_id=1, source_target_pairs={{0,24},{4,28},{8,16},{12,20},{16,8},{20,12},{24,0},{28,4},{1,25},{... | collective-permute-start | bytes 1179656 | tf_op jit(solution)/shard_map/ppermute | solution.py:582
  101.5 82.0 %collective-permute-start.10 = (f32[12,64,128]{2,1,0:T(8,128)S(1)}, f32[12,64,128]{2,1,0:T(8,128)S(1)}, u32[]{:S(2)}, u32[]{:S(2)}) collective-permute-start(f32[12,64,128]{2,1,0:T(8,128)S(1)} %copy-done.183), channel_id=1, source_target_pairs={{0,28},{4,24},{8,20},{12,16},{16,12},{20,8},{24,4},{28,0},{1,29},{... | collective-permute-start | bytes 1179656 | tf_op jit(solution)/shard_map/ppermute | solution.py:582
  103.9 80.3 %collective-permute-start.11 = (f32[12,64,128]{2,1,0:T(8,128)S(1)}, f32[12,64,128]{2,1,0:T(8,128)S(1)}, u32[]{:S(2)}, u32[]{:S(2)}) collective-permute-start(f32[12,64,128]{2,1,0:T(8,128)S(1)} %copy-done.114), channel_id=1, source_target_pairs={{0,4},{4,0},{8,12},{12,8},{16,20},{20,16},{24,28},{28,24},{1,5},{5... | collective-permute-start | bytes 1179656 | tf_op jit(solution)/shard_map/ppermute | solution.py:582
  127.3 59.0 %collective-permute-start.12 = (f32[12,64,128]{2,1,0:T(8,128)S(1)}, f32[12,64,128]{2,1,0:T(8,128)S(1)}, u32[]{:S(2)}, u32[]{:S(2)}) collective-permute-start(f32[12,64,128]{2,1,0:T(8,128)S(1)} %get-tuple-element.149), channel_id=1, source_target_pairs={{0,8},{4,12},{8,0},{12,4},{16,24},{20,28},{24,16},{28,20},{1,9},{5... | collective-permute-start | bytes 1179656 | tf_op jit(solution)/shard_map/ppermute | solution.py:582
  133.8 67.1 %collective-permute-start.13 = (f32[12,64,128]{2,1,0:T(8,128)}, f32[12,64,128]{2,1,0:T(8,128)S(1)}, u32[]{:S(2)}, u32[]{:S(2)}) collective-permute-start(f32[12,64,128]{2,1,0:T(8,128)} %get-tuple-element.150), channel_id=1, source_target_pairs={{0,12},{4,8},{8,4},{12,0},{16,28},{20,24},{24,20},{28,16},{1,13},{... | collective-permute-start | bytes 1179656 | tf_op jit(solution)/shard_map/ppermute | solution.py:582
  186.3 71.5 %collective-permute-start.17 = (f32[12,64,128]{2,1,0:T(8,128)S(1)}, f32[12,64,128]{2,1,0:T(8,128)S(1)}, u32[]{:S(2)}, u32[]{:S(2)}) collective-permute-start(f32[12,64,128]{2,1,0:T(8,128)S(1)} %get-tuple-element.154), channel_id=1, source_target_pairs={{0,28},{4,24},{8,20},{12,16},{16,12},{20,8},{24,4},{28,0},{1,29},{... | collective-permute-start | bytes 1179656 | tf_op jit(solution)/shard_map/ppermute | solution.py:582
  200.8 67.5 %collective-permute-start.21 = (f32[12,64,128]{2,1,0:T(8,128)S(1)}, f32[12,64,128]{2,1,0:T(8,128)S(1)}, u32[]{:S(2)}, u32[]{:S(2)}) collective-permute-start(f32[12,64,128]{2,1,0:T(8,128)S(1)} %get-tuple-element.160), channel_id=1, source_target_pairs={{0,4},{4,0},{8,12},{12,8},{16,20},{20,16},{24,28},{28,24},{1,5},{5... | collective-permute-start | bytes 1179656 | tf_op jit(solution)/shard_map/ppermute | solution.py:582
  226.6 59.1 %collective-permute-start.18 = (f32[16,96,128]{2,1,0:T(8,128)}, f32[16,96,128]{2,1,0:T(8,128)}, u32[]{:S(2)}, u32[]{:S(2)}) collective-permute-start(f32[16,96,128]{2,1,0:T(8,128)} %get-tuple-element.156), channel_id=1, source_target_pairs={{0,1},{1,0},{2,3},{3,2},{4,5},{5,4},{6,7},{7,6},{8,9},{9,8},{10,11... | collective-permute-start | bytes 2359304 | tf_op jit(solution)/shard_map/ppermute | solution.py:582
  276.0 73.8 %collective-permute-start.28 = (f32[16,96,128]{2,1,0:T(8,128)}, f32[16,96,128]{2,1,0:T(8,128)}, u32[]{:S(2)}, u32[]{:S(2)}) collective-permute-start(f32[16,96,128]{2,1,0:T(8,128)} %get-tuple-element.168), channel_id=1, source_target_pairs={{0,1},{1,0},{2,3},{3,2},{4,5},{5,4},{6,7},{7,6},{8,9},{9,8},{10,11... | collective-permute-start | bytes 2359304 | tf_op jit(solution)/shard_map/ppermute | solution.py:582
  606.4 60.4 %collective-permute-start.58 = (f32[16,96,128]{2,1,0:T(8,128)S(1)}, f32[16,96,128]{2,1,0:T(8,128)S(1)}, u32[]{:S(2)}, u32[]{:S(2)}) collective-permute-start(f32[16,96,128]{2,1,0:T(8,128)S(1)} %get-tuple-element.201), channel_id=1, source_target_pairs={{0,2},{1,3},{2,0},{3,1},{4,6},{5,7},{6,4},{7,5},{8,10},{9,11},{10,... | collective-permute-start | bytes 2359304 | tf_op jit(solution)/shard_map/ppermute | solution.py:582
  607.8 61.2 %collective-permute-start.59 = (f32[16,96,128]{2,1,0:T(8,128)S(1)}, f32[16,96,128]{2,1,0:T(8,128)S(1)}, u32[]{:S(2)}, u32[]{:S(2)}) collective-permute-start(f32[16,96,128]{2,1,0:T(8,128)S(1)} %get-tuple-element.202), channel_id=1, source_target_pairs={{0,3},{1,2},{2,1},{3,0},{4,7},{5,6},{6,5},{7,4},{8,11},{9,10},{10,... | collective-permute-start | bytes 2359304 | tf_op jit(solution)/shard_map/ppermute | solution.py:582
  634.9 60.0 %collective-permute-start.66 = (f32[12,64,128]{2,1,0:T(8,128)S(1)}, f32[12,64,128]{2,1,0:T(8,128)S(1)}, u32[]{:S(2)}, u32[]{:S(2)}) collective-permute-start(f32[12,64,128]{2,1,0:T(8,128)S(1)} %copy-done.65), channel_id=1, source_target_pairs={{0,16},{4,20},{8,24},{12,28},{16,0},{20,4},{24,8},{28,12},{1,17},{... | collective-permute-start | bytes 1179656 | tf_op jit(solution)/shard_map/ppermute | solution.py:582
  635.8 59.7 %collective-permute-start.67 = (f32[12,64,128]{2,1,0:T(8,128)S(1)}, f32[12,64,128]{2,1,0:T(8,128)S(1)}, u32[]{:S(2)}, u32[]{:S(2)}) collective-permute-start(f32[12,64,128]{2,1,0:T(8,128)S(1)} %copy-done.63), channel_id=1, source_target_pairs={{0,20},{4,16},{8,28},{12,24},{16,4},{20,0},{24,12},{28,8},{1,21},{... | collective-permute-start | bytes 1179656 | tf_op jit(solution)/shard_map/ppermute | solution.py:582
  798.6 64.4 %collective-permute-start.79 = (f32[8,96,128]{2,1,0:T(8,128)}, f32[8,96,128]{2,1,0:T(8,128)S(1)}, u32[]{:S(2)}, u32[]{:S(2)}) collective-permute-start(f32[8,96,128]{2,1,0:T(8,128)} %copy-done.123), channel_id=1, source_target_pairs={{0,1},{1,0},{2,3},{3,2},{4,5},{5,4},{6,7},{7,6},{8,9},{9,8},{10,11... | collective-permute-start | bytes 1179656 | tf_op jit(solution)/shard_map/ppermute | solution.py:582
  908.2 59.7 %collective-permute-start.93 = (f32[12,64,128]{2,1,0:T(8,128)S(1)}, f32[12,64,128]{2,1,0:T(8,128)S(1)}, u32[]{:S(2)}, u32[]{:S(2)}) collective-permute-start(f32[12,64,128]{2,1,0:T(8,128)S(1)} %get-tuple-element.243), channel_id=1, source_target_pairs={{0,8},{4,12},{8,0},{12,4},{16,24},{20,28},{24,16},{28,20},{1,9},{5... | collective-permute-start | bytes 1179656 | tf_op jit(solution)/shard_map/ppermute | solution.py:582
  938.1 86.8 %collective-permute-start.94 = (f32[12,64,128]{2,1,0:T(8,128)S(1)}, f32[12,64,128]{2,1,0:T(8,128)}, u32[]{:S(2)}, u32[]{:S(2)}) collective-permute-start(f32[12,64,128]{2,1,0:T(8,128)S(1)} %get-tuple-element.244), channel_id=1, source_target_pairs={{0,12},{4,8},{8,4},{12,0},{16,28},{20,24},{24,20},{28,16},{1,13},{... | collective-permute-start | bytes 1179656 | tf_op jit(solution)/shard_map/ppermute | solution.py:582
  938.1 86.8 %collective-permute-start.95 = (f32[12,64,128]{2,1,0:T(8,128)S(1)}, f32[12,64,128]{2,1,0:T(8,128)}, u32[]{:S(2)}, u32[]{:S(2)}) collective-permute-start(f32[12,64,128]{2,1,0:T(8,128)S(1)} %get-tuple-element.245), channel_id=1, source_target_pairs={{0,16},{4,20},{8,24},{12,28},{16,0},{20,4},{24,8},{28,12},{1,17},{... | collective-permute-start | bytes 1179656 | tf_op jit(solution)/shard_map/ppermute | solution.py:582
  949.6 75.3 %collective-permute-start.96 = (f32[12,64,128]{2,1,0:T(8,128)S(1)}, f32[12,64,128]{2,1,0:T(8,128)}, u32[]{:S(2)}, u32[]{:S(2)}) collective-permute-start(f32[12,64,128]{2,1,0:T(8,128)S(1)} %get-tuple-element.246), channel_id=1, source_target_pairs={{0,20},{4,16},{8,28},{12,24},{16,4},{20,0},{24,12},{28,8},{1,21},{... | collective-permute-start | bytes 1179656 | tf_op jit(solution)/shard_map/ppermute | solution.py:582
  965.9 59.0 %collective-permute-start.97 = (f32[12,64,128]{2,1,0:T(8,128)S(1)}, f32[12,64,128]{2,1,0:T(8,128)}, u32[]{:S(2)}, u32[]{:S(2)}) collective-permute-start(f32[12,64,128]{2,1,0:T(8,128)S(1)} %get-tuple-element.247), channel_id=1, source_target_pairs={{0,24},{4,28},{8,16},{12,20},{16,8},{20,12},{24,0},{28,4},{1,25},{... | collective-permute-start | bytes 1179656 | tf_op jit(solution)/shard_map/ppermute | solution.py:582
  (276 other events, 5955.7 us)

commit v3 on v2

--- a/solution.py
+++ b/solution.py
@@ -407,8 +407,10 @@
     pl.when(step == 0)(lambda: take(front_ref))
     pl.when(step == last)(lambda: take(back_ref))
     pl.when(jnp.logical_and(step > 0, step < last))(lambda: take(own_ref))
-    for p in range(STRIDE):
-        planes[p * tall + columns : (p + 1) * tall, :] = edge_ref[p]
+
+    @pl.loop(0, STRIDE)
+    def _(p):
+        planes[pl.ds(pl.multiple_of(p * tall + columns, 8), edges), :] = edge_ref[p]
 
     high, low = halves(planes[...])
     mass, stiff = [], []
@@ -444,15 +446,20 @@
         @pl.loop(0, STRIDE)
         def _(p):
             row = STRIDE * (step - 2) + p
-            total = reaction_ref[p] * direction_ref[p]
-            for o in range(7):
-                place = lax.rem(row + o + STRIDE - 3, RING)
-                total = total + (
-                    coefficient_ref[row * 14 + o] * mass_ring[place]
-                    + coefficient_ref[row * 14 + 7 + o] * stiff_ring[place]
-                )
-            image_ref[p] = total
-            sum_ref[...] += folded(direction_ref[p] * total)
+
+            @pl.loop(0, columns // 16)
+            def _(tile):
+                lines = pl.ds(pl.multiple_of(tile * 16, 16), 16)
+                own = direction_ref[p, lines, :]
+                total = reaction_ref[p, lines, :] * own
+                for o in range(7):
+                    place = lax.rem(row + o + STRIDE - 3, RING)
+                    total = total + (
+                        coefficient_ref[row * 14 + o] * mass_ring[place, lines, :]
+                        + coefficient_ref[row * 14 + 7 + o] * stiff_ring[place, lines, :]
+                    )
+                image_ref[p, lines, :] = total
+                sum_ref[...] += folded(own * total)
 
 
 def neighbours(head, tail, axis):

time: 1050 us -> 1060 us (level)
  no operation moved by 1% of the time
where the time goes in v3:
time: 1060 us; the launch traced here: 1050 us
  waiting for transfers between devices  382 us (36%)
  Pallas kernels  307 us (29%)
  starting transfers between devices  243 us (23%)
  local copies, waits for them, and re-layouts  77.8 us (7%)
  other arithmetic  30.9 us (3%)
    ppermute x109, waiting for transfers between devices, by_xor(): lax.ppermute(block, axis, [(j, j ^ k) for j in range(lax.axis_size(axis))])  369 us
    pallas_call x27, Pallas kernels, ordered_call(): return lambda *args: call(*after, *args)  307 us
    ppermute x109, starting transfers between devices, by_xor(): lax.ppermute(block, axis, [(j, j ^ k) for j in range(lax.axis_size(axis))])  237 us
    unnamed x384, local copies, waits for them, and re-layouts  60.8 us
  transfers between devices with their start and end apart: 113, of which 31 were waited for; matrix products, arithmetic and copies ran while one was open for 5% of the time, Pallas kernels for 27%

profile of v3, /device:TPU:0, one launch (start us, length us, event | category | flops | bytes accessed | tf_op | source)
XLA Modules:
  0.0 1049.3 jit_solution(6177646265785603897)
XLA Ops:
  6.3 13.4 %y_forward.6 = (f32[12,64,128]{2,1,0:T(8,128)}, f32[12,64,128]{2,1,0:T(8,128)}, f32[12,64,128]{2,1,0:T(8,128)}, f32[12,64,128]{2,1,0:T(8,128)}, f32[12,64,128]{2...) custom-call(f32[64,96,384]{2,1,0:T(8,128)} %refs_3_.1, ...), custom_call_target="tpu_custom_call" | custom-call | flops 1811939328 | bytes 12582912 | tf_op jit(solution)/shard_map/y_forward/pallas_call | solution.py:36
  104.1 22.4 %collective-permute-done.7.refs_6_ = f32[12,64,128]{2,1,0:T(8,128)S(1)} collective-permute-done((f32[12,64,128]{2,1,0:T(8,128)S(1)}, f32[12,64,128]{2,1,0:T(8,128)S(1)}, u32[]{:S(2)}, u32[]{:S(2)}) %collective-permute-start.7) | collective-permute-done | bytes 393248 | tf_op jit(solution)/shard_map/ppermute | solution.py:589
  133.8 52.8 %image.1 = (f32[64,96,384]{2,1,0:T(8,128)}, f32[8,384]{1,0:T(8,128)}) custom-call(f32[12,64,128]{2,1,0:T(8,128)} %copy-done.84, f32[896]{0:T(1024)} %reshape.112.refs_1_, f32[4,96,384]{2,1,0:T(8,128)} %concatenate.90.refs_2_, f32[4,96,384]{2,1,0:T(8,128)} %concatenate.91.refs_3_, f32[64,96,384]{2,1,0:T(8,128)} %refs_19_.1, ...), custom_call_target="tpu_custom_call" | custom-call | flops 13872660480 | bytes 37748736 | tf_op jit(solution)/shard_map/image/pallas_call | solution.py:36
  309.9 29.5 %collective-permute-done.24.refs_6_ = f32[12,64,128]{2,1,0:T(8,128)S(1)} collective-permute-done((f32[12,64,128]{2,1,0:T(8,128)}, f32[12,64,128]{2,1,0:T(8,128)S(1)}, u32[]{:S(2)}, u32[]{:S(2)}) %collective-permute-start.24) | collective-permute-done | bytes 393248 | tf_op jit(solution)/shard_map/ppermute | solution.py:589
  361.8 15.7 %collective-permute-done.29.refs_4_ = f32[16,96,128]{2,1,0:T(8,128)} collective-permute-done((f32[16,96,128]{2,1,0:T(8,128)}, f32[16,96,128]{2,1,0:T(8,128)}, u32[]{:S(2)}, u32[]{:S(2)}) %collective-permute-start.29) | collective-permute-done | bytes 786464 | tf_op jit(solution)/shard_map/ppermute | solution.py:589
  391.1 19.3 %collective-permute-done.32.refs_4_ = f32[16,96,128]{2,1,0:T(8,128)} collective-permute-done((f32[16,96,128]{2,1,0:T(8,128)}, f32[16,96,128]{2,1,0:T(8,128)}, u32[]{:S(2)}, u32[]{:S(2)}) %collective-permute-start.32) | collective-permute-done | bytes 786464 | tf_op jit(solution)/shard_map/ppermute | solution.py:589
  444.7 28.3 %collective-permute-done.37.refs_6_ = f32[12,64,128]{2,1,0:T(8,128)S(1)} collective-permute-done((f32[12,64,128]{2,1,0:T(8,128)}, f32[12,64,128]{2,1,0:T(8,128)S(1)}, u32[]{:S(2)}, u32[]{:S(2)}) %collective-permute-start.37) | collective-permute-done | bytes 393248 | tf_op jit(solution)/shard_map/ppermute | solution.py:589
  494.4 16.4 %collective-permute-start.46 = (f32[8,128]{1,0:T(8,128)S(1)}, f32[8,128]{1,0:T(8,128)S(1)}, u32[]{:S(2)}, u32[]{:S(2)}) collective-permute-start(f32[8,128]{1,0:T(8,128)S(1)} %add.142), channel_id=1, source_target_pairs={{0,8},{4,12},{8,0},{12,4},{16,24},{20,28},{24,16},{28,20},{1,9},{5... | collective-permute-start | bytes 12296 | tf_op jit(solution)/shard_map/ppermute | solution.py:589
  518.3 15.8 %collective-permute-done.51.refs_4_ = f32[12,64,128]{2,1,0:T(8,128)S(1)} collective-permute-done((f32[12,64,128]{2,1,0:T(8,128)S(1)}, f32[12,64,128]{2,1,0:T(8,128)S(1)}, u32[]{:S(2)}, u32[]{:S(2)}) %collective-permute-start.51) | collective-permute-done | bytes 393248 | tf_op jit(solution)/shard_map/ppermute | solution.py:589
  542.2 17.1 %x_second.4 = (f32[16,96,128]{2,1,0:T(8,128)S(1)}, f32[16,96,128]{2,1,0:T(8,128)S(1)}, f32[16,96,128]{2,1,0:T(8,128)S(1)}, f32[16,96,128]{2,1,0:T(8,128)S(1)}, f32[8,256]{1,0:T(8,128)S(1)}) custom-call(f32[16,96,128]{2,1,0:T(8,128)S(1)} %get-tuple-element.183.refs_0_.refs_3_, s32[2]{0:T(128)S(1)} %pad_add_fusion.1.refs_1_, f32[1]{0:T(128)} %bitcast.41.refs_2_.refs_1_, ...), custom_call_target="tpu_custom_call" | custom-call | flops 3623878656 | bytes 9437184 | tf_op jit(solution)/shard_map/x_second/pallas_call | solution.py:36
  559.3 19.1 %collective-permute-done.53.refs_6_ = f32[12,64,128]{2,1,0:T(8,128)S(1)} collective-permute-done((f32[12,64,128]{2,1,0:T(8,128)S(1)}, f32[12,64,128]{2,1,0:T(8,128)S(1)}, u32[]{:S(2)}, u32[]{:S(2)}) %collective-permute-start.53) | collective-permute-done | bytes 393248 | tf_op jit(solution)/shard_map/ppermute | solution.py:589
  592.2 13.1 %collective-permute-start.64 = (f32[12,64,128]{2,1,0:T(8,128)S(1)}, f32[12,64,128]{2,1,0:T(8,128)S(1)}, u32[]{:S(2)}, u32[]{:S(2)}) collective-permute-start(f32[12,64,128]{2,1,0:T(8,128)S(1)} %copy-done.69), channel_id=1, source_target_pairs={{0,8},{4,12},{8,0},{12,4},{16,24},{20,28},{24,16},{28,20},{1,9},{5... | collective-permute-start | bytes 1179656 | tf_op jit(solution)/shard_map/ppermute | solution.py:589
  618.0 25.2 %collective-permute-done.61.refs_5_ = f32[16,96,128]{2,1,0:T(8,128)S(1)} collective-permute-done((f32[16,96,128]{2,1,0:T(8,128)S(1)}, f32[16,96,128]{2,1,0:T(8,128)S(1)}, u32[]{:S(2)}, u32[]{:S(2)}) %collective-permute-start.61) | collective-permute-done | bytes 786464 | tf_op jit(solution)/shard_map/ppermute | solution.py:589
  644.1 14.2 %collective-permute-start.67 = (f32[12,64,128]{2,1,0:T(8,128)S(1)}, f32[12,64,128]{2,1,0:T(8,128)S(1)}, u32[]{:S(2)}, u32[]{:S(2)}) collective-permute-start(f32[12,64,128]{2,1,0:T(8,128)S(1)} %copy-done.63), channel_id=1, source_target_pairs={{0,20},{4,16},{8,28},{12,24},{16,4},{20,0},{24,12},{28,8},{1,21},{... | collective-permute-start | bytes 1179656 | tf_op jit(solution)/shard_map/ppermute | solution.py:589
  658.3 16.9 %collective-permute-done.58.refs_4_ = f32[16,96,128]{2,1,0:T(8,128)S(1)} collective-permute-done((f32[16,96,128]{2,1,0:T(8,128)S(1)}, f32[16,96,128]{2,1,0:T(8,128)S(1)}, u32[]{:S(2)}, u32[]{:S(2)}) %collective-permute-start.58) | collective-permute-done | bytes 786464 | tf_op jit(solution)/shard_map/ppermute | solution.py:589
  683.8 17.8 %x_second.5 = (f32[16,96,128]{2,1,0:T(8,128)S(1)}, f32[16,96,128]{2,1,0:T(8,128)}, f32[16,96,128]{2,1,0:T(8,128)}, f32[16,96,128]{2,1,0:T(8,128)}, f32[8,256]{1,0:T(8,128)S(1)}) custom-call(f32[12,64,128]{2,1,0:T(8,128)S(1)} %get-tuple-element.203.refs_0_.refs_2_, s32[2]{0:T(128)S(1)} %pad_add_fusion.1.refs_1_, f32[1]{0:T(128)} %bitcast.41.refs_2_.refs_1_, ...), custom_call_target="tpu_custom_call" | custom-call | flops 3623878656 | bytes 9437184 | tf_op jit(solution)/shard_map/x_second/pallas_call | solution.py:36
  716.8 30.0 %collective-permute-done.73.refs_4_ = f32[8,96,128]{2,1,0:T(8,128)S(1)} collective-permute-done((f32[8,96,128]{2,1,0:T(8,128)S(1)}, f32[8,96,128]{2,1,0:T(8,128)S(1)}, u32[]{:S(2)}, u32[]{:S(2)}) %collective-permute-start.73) | collective-permute-done | bytes 393248 | tf_op jit(solution)/shard_map/ppermute | solution.py:589
  808.3 36.4 %collective-permute-done.102.refs_6_ = f32[12,64,128]{2,1,0:T(8,128)} collective-permute-done((f32[12,64,128]{2,1,0:T(8,128)}, f32[12,64,128]{2,1,0:T(8,128)}, u32[]{:S(2)}, u32[]{:S(2)}) %collective-permute-start.102) | collective-permute-done | bytes 393248 | tf_op jit(solution)/shard_map/ppermute | solution.py:589
  856.7 13.4 %collective-permute-done.90.refs_4_ = f32[8,128]{1,0:T(8,128)S(1)} collective-permute-done((f32[8,128]{1,0:T(8,128)S(1)}, f32[8,128]{1,0:T(8,128)S(1)}, u32[]{:S(2)}, u32[]{:S(2)}) %collective-permute-start.90) | collective-permute-done | bytes 4128 | tf_op jit(solution)/shard_map/ppermute | solution.py:589
  917.5 28.9 %collective-permute-done.110.refs_15_ = f32[12,64,128]{2,1,0:T(8,128)S(1)} collective-permute-done((f32[12,64,128]{2,1,0:T(8,128)S(1)}, f32[12,64,128]{2,1,0:T(8,128)S(1)}, u32[]{:S(2)}, u32[]{:S(2)}) %collective-permute-start.110) | collective-permute-done | bytes 393248 | tf_op jit(solution)/shard_map/ppermute | solution.py:589
  957.9 16.3 %collective-permute-start.96 = (f32[12,64,128]{2,1,0:T(8,128)S(1)}, f32[12,64,128]{2,1,0:T(8,128)}, u32[]{:S(2)}, u32[]{:S(2)}) collective-permute-start(f32[12,64,128]{2,1,0:T(8,128)S(1)} %get-tuple-element.246), channel_id=1, source_target_pairs={{0,20},{4,16},{8,28},{12,24},{16,4},{20,0},{24,12},{28,8},{1,21},{... | collective-permute-start | bytes 1179656 | tf_op jit(solution)/shard_map/ppermute | solution.py:589
  981.1 28.0 %update.1 = (f32[64,96,384]{2,1,0:T(8,128)}, f32[64,96,384]{2,1,0:T(8,128)}) custom-call(f32[12,64,128]{2,1,0:T(8,128)S(1)} %get-tuple-element.235.refs_0_.refs_1_, f32[1]{0:T(128)} %bitcast.41.refs_2_.refs_1_, f32[64,96,384]{2,1,0:T(8,128)S(1)} %copy-done.5, f32[64,96,384]{2,1,0:T(8,128)} %refs_3_.1, f32[64,96,384]{2,1,0:T(8,128)} %refs_19_.1, ...), custom_call_target="tpu_custom_call" | custom-call | flops 9437184 | bytes 56623104 | tf_op jit(solution)/shard_map/update/pallas_call | solution.py:36
  1014.1 19.1 %y_inverse.2.refs_10_ = f32[64,96,384]{2,1,0:T(8,128)} custom-call(f32[8,128]{1,0:T(8,128)} %copy-done.47, f32[1]{0:T(128)} %bitcast.43.refs_1_.refs_0_, f32[12,64,128]{2,1,0:T(8,128)} %copy-done.46, f32[12,64,128]{2,1,0:T(8,128)} %collective-permute-done.99.refs_3_, f32[12,64,128]{2,1,0:T(8,128)} %collective-permute-done.100.refs_4_, ...), custom_call_target="tpu_custom_call" | custom-call | flops 3623878656 | bytes 25165824 | tf_op jit(solution)/shard_map/y_inverse/pallas_call | solution.py:36
  1033.3 15.8 %y_inverse.3 = f32[64,96,384]{2,1,0:T(8,128)} custom-call(f32[1]{0:T(128)} %bitcast.43.refs_1_.refs_0_, f32[12,64,128]{2,1,0:T(8,128)} %copy-done.17, f32[12,64,128]{2,1,0:T(8,128)} %copy-done.160, f32[12,64,128]{2,1,0:T(8,128)} %copy-done.162, f32[12,64,128]{2,1,0:T(8,128)} %collective-permute-done.94.refs_4_, ...), custom_call_target="tpu_custom_call", output_to_operand_aliasing={{}: (10, {})} | custom-call | flops 1811939328 | bytes 22020096 | tf_op jit(solution)/shard_map/y_inverse/pallas_call | solution.py:36
  (705 shorter events, 515.9 us)
Async XLA Ops:
  2.8 65.0 %collective-permute-start.1 = (f32[3,96,384]{2,1,0:T(8,128)}, f32[3,96,384]{2,1,0:T(8,128)}, u32[]{:S(2)}, u32[]{:S(2)}) collective-permute-start(f32[3,96,384]{2,1,0:T(8,128)} %get-tuple-element.273), channel_id=1, source_target_pairs={{0,4},{8,12},{16,20},{24,28},{4,0},{12,8},{20,16},{28,24},{1,5},{9... | collective-permute-start | bytes 1327112 | tf_op jit(solution)/shard_map/ppermute | solution.py:471
  3.3 64.5 %collective-permute-start = (f32[3,96,384]{2,1,0:T(8,128)}, f32[3,96,384]{2,1,0:T(8,128)}, u32[]{:S(2)}, u32[]{:S(2)}) collective-permute-start(f32[3,96,384]{2,1,0:T(8,128)} %get-tuple-element.274), channel_id=1, source_target_pairs={{4,8},{12,16},{20,24},{8,4},{16,12},{24,20},{5,9},{13,17},{21,25},... | collective-permute-start | bytes 1327112 | tf_op jit(solution)/shard_map/ppermute | solution.py:471
  19.7 80.3 %collective-permute-start.4 = (f32[12,64,128]{2,1,0:T(8,128)}, f32[12,64,128]{2,1,0:T(8,128)S(1)}, u32[]{:S(2)}, u32[]{:S(2)}) collective-permute-start(f32[12,64,128]{2,1,0:T(8,128)} %get-tuple-element.137), channel_id=1, source_target_pairs={{0,4},{4,0},{8,12},{12,8},{16,20},{20,16},{24,28},{28,24},{1,5},{5... | collective-permute-start | bytes 1179656 | tf_op jit(solution)/shard_map/ppermute | solution.py:589
  22.9 78.5 %collective-permute-start.5 = (f32[12,64,128]{2,1,0:T(8,128)}, f32[12,64,128]{2,1,0:T(8,128)}, u32[]{:S(2)}, u32[]{:S(2)}) collective-permute-start(f32[12,64,128]{2,1,0:T(8,128)} %get-tuple-element.138), channel_id=1, source_target_pairs={{0,8},{4,12},{8,0},{12,4},{16,24},{20,28},{24,16},{28,20},{1,9},{5... | collective-permute-start | bytes 1179656 | tf_op jit(solution)/shard_map/ppermute | solution.py:589
  24.5 79.4 %collective-permute-start.6 = (f32[12,64,128]{2,1,0:T(8,128)}, f32[12,64,128]{2,1,0:T(8,128)}, u32[]{:S(2)}, u32[]{:S(2)}) collective-permute-start(f32[12,64,128]{2,1,0:T(8,128)} %get-tuple-element.139), channel_id=1, source_target_pairs={{0,12},{4,8},{8,4},{12,0},{16,28},{20,24},{24,20},{28,16},{1,13},{... | collective-permute-start | bytes 1179656 | tf_op jit(solution)/shard_map/ppermute | solution.py:589
  100.0 86.5 %collective-permute-start.9 = (f32[12,64,128]{2,1,0:T(8,128)S(1)}, f32[12,64,128]{2,1,0:T(8,128)S(1)}, u32[]{:S(2)}, u32[]{:S(2)}) collective-permute-start(f32[12,64,128]{2,1,0:T(8,128)S(1)} %copy-done.184), channel_id=1, source_target_pairs={{0,24},{4,28},{8,16},{12,20},{16,8},{20,12},{24,0},{28,4},{1,25},{... | collective-permute-start | bytes 1179656 | tf_op jit(solution)/shard_map/ppermute | solution.py:589
  101.5 90.3 %collective-permute-start.10 = (f32[12,64,128]{2,1,0:T(8,128)S(1)}, f32[12,64,128]{2,1,0:T(8,128)S(1)}, u32[]{:S(2)}, u32[]{:S(2)}) collective-permute-start(f32[12,64,128]{2,1,0:T(8,128)S(1)} %copy-done.183), channel_id=1, source_target_pairs={{0,28},{4,24},{8,20},{12,16},{16,12},{20,8},{24,4},{28,0},{1,29},{... | collective-permute-start | bytes 1179656 | tf_op jit(solution)/shard_map/ppermute | solution.py:589
  103.9 88.6 %collective-permute-start.11 = (f32[12,64,128]{2,1,0:T(8,128)S(1)}, f32[12,64,128]{2,1,0:T(8,128)S(1)}, u32[]{:S(2)}, u32[]{:S(2)}) collective-permute-start(f32[12,64,128]{2,1,0:T(8,128)S(1)} %copy-done.114), channel_id=1, source_target_pairs={{0,4},{4,0},{8,12},{12,8},{16,20},{20,16},{24,28},{28,24},{1,5},{5... | collective-permute-start | bytes 1179656 | tf_op jit(solution)/shard_map/ppermute | solution.py:589
  127.3 67.3 %collective-permute-start.12 = (f32[12,64,128]{2,1,0:T(8,128)S(1)}, f32[12,64,128]{2,1,0:T(8,128)S(1)}, u32[]{:S(2)}, u32[]{:S(2)}) collective-permute-start(f32[12,64,128]{2,1,0:T(8,128)S(1)} %get-tuple-element.149), channel_id=1, source_target_pairs={{0,8},{4,12},{8,0},{12,4},{16,24},{20,28},{24,16},{28,20},{1,9},{5... | collective-permute-start | bytes 1179656 | tf_op jit(solution)/shard_map/ppermute | solution.py:589
  133.8 75.4 %collective-permute-start.13 = (f32[12,64,128]{2,1,0:T(8,128)}, f32[12,64,128]{2,1,0:T(8,128)S(1)}, u32[]{:S(2)}, u32[]{:S(2)}) collective-permute-start(f32[12,64,128]{2,1,0:T(8,128)} %get-tuple-element.150), channel_id=1, source_target_pairs={{0,12},{4,8},{8,4},{12,0},{16,28},{20,24},{24,20},{28,16},{1,13},{... | collective-permute-start | bytes 1179656 | tf_op jit(solution)/shard_map/ppermute | solution.py:589
  194.6 71.5 %collective-permute-start.17 = (f32[12,64,128]{2,1,0:T(8,128)S(1)}, f32[12,64,128]{2,1,0:T(8,128)S(1)}, u32[]{:S(2)}, u32[]{:S(2)}) collective-permute-start(f32[12,64,128]{2,1,0:T(8,128)S(1)} %get-tuple-element.154), channel_id=1, source_target_pairs={{0,28},{4,24},{8,20},{12,16},{16,12},{20,8},{24,4},{28,0},{1,29},{... | collective-permute-start | bytes 1179656 | tf_op jit(solution)/shard_map/ppermute | solution.py:589
  209.2 67.5 %collective-permute-start.21 = (f32[12,64,128]{2,1,0:T(8,128)S(1)}, f32[12,64,128]{2,1,0:T(8,128)S(1)}, u32[]{:S(2)}, u32[]{:S(2)}) collective-permute-start(f32[12,64,128]{2,1,0:T(8,128)S(1)} %get-tuple-element.160), channel_id=1, source_target_pairs={{0,4},{4,0},{8,12},{12,8},{16,20},{20,16},{24,28},{28,24},{1,5},{5... | collective-permute-start | bytes 1179656 | tf_op jit(solution)/shard_map/ppermute | solution.py:589
  234.9 59.1 %collective-permute-start.18 = (f32[16,96,128]{2,1,0:T(8,128)}, f32[16,96,128]{2,1,0:T(8,128)}, u32[]{:S(2)}, u32[]{:S(2)}) collective-permute-start(f32[16,96,128]{2,1,0:T(8,128)} %get-tuple-element.156), channel_id=1, source_target_pairs={{0,1},{1,0},{2,3},{3,2},{4,5},{5,4},{6,7},{7,6},{8,9},{9,8},{10,11... | collective-permute-start | bytes 2359304 | tf_op jit(solution)/shard_map/ppermute | solution.py:589
  284.3 73.8 %collective-permute-start.28 = (f32[16,96,128]{2,1,0:T(8,128)}, f32[16,96,128]{2,1,0:T(8,128)}, u32[]{:S(2)}, u32[]{:S(2)}) collective-permute-start(f32[16,96,128]{2,1,0:T(8,128)} %get-tuple-element.168), channel_id=1, source_target_pairs={{0,1},{1,0},{2,3},{3,2},{4,5},{5,4},{6,7},{7,6},{8,9},{9,8},{10,11... | collective-permute-start | bytes 2359304 | tf_op jit(solution)/shard_map/ppermute | solution.py:589
  614.7 60.4 %collective-permute-start.58 = (f32[16,96,128]{2,1,0:T(8,128)S(1)}, f32[16,96,128]{2,1,0:T(8,128)S(1)}, u32[]{:S(2)}, u32[]{:S(2)}) collective-permute-start(f32[16,96,128]{2,1,0:T(8,128)S(1)} %get-tuple-element.201), channel_id=1, source_target_pairs={{0,2},{1,3},{2,0},{3,1},{4,6},{5,7},{6,4},{7,5},{8,10},{9,11},{10,... | collective-permute-start | bytes 2359304 | tf_op jit(solution)/shard_map/ppermute | solution.py:589
  616.1 61.2 %collective-permute-start.59 = (f32[16,96,128]{2,1,0:T(8,128)S(1)}, f32[16,96,128]{2,1,0:T(8,128)S(1)}, u32[]{:S(2)}, u32[]{:S(2)}) collective-permute-start(f32[16,96,128]{2,1,0:T(8,128)S(1)} %get-tuple-element.202), channel_id=1, source_target_pairs={{0,3},{1,2},{2,1},{3,0},{4,7},{5,6},{6,5},{7,4},{8,11},{9,10},{10,... | collective-permute-start | bytes 2359304 | tf_op jit(solution)/shard_map/ppermute | solution.py:589
  643.2 60.0 %collective-permute-start.66 = (f32[12,64,128]{2,1,0:T(8,128)S(1)}, f32[12,64,128]{2,1,0:T(8,128)S(1)}, u32[]{:S(2)}, u32[]{:S(2)}) collective-permute-start(f32[12,64,128]{2,1,0:T(8,128)S(1)} %copy-done.65), channel_id=1, source_target_pairs={{0,16},{4,20},{8,24},{12,28},{16,0},{20,4},{24,8},{28,12},{1,17},{... | collective-permute-start | bytes 1179656 | tf_op jit(solution)/shard_map/ppermute | solution.py:589
  644.1 59.6 %collective-permute-start.67 = (f32[12,64,128]{2,1,0:T(8,128)S(1)}, f32[12,64,128]{2,1,0:T(8,128)S(1)}, u32[]{:S(2)}, u32[]{:S(2)}) collective-permute-start(f32[12,64,128]{2,1,0:T(8,128)S(1)} %copy-done.63), channel_id=1, source_target_pairs={{0,20},{4,16},{8,28},{12,24},{16,4},{20,0},{24,12},{28,8},{1,21},{... | collective-permute-start | bytes 1179656 | tf_op jit(solution)/shard_map/ppermute | solution.py:589
  806.9 64.4 %collective-permute-start.79 = (f32[8,96,128]{2,1,0:T(8,128)}, f32[8,96,128]{2,1,0:T(8,128)S(1)}, u32[]{:S(2)}, u32[]{:S(2)}) collective-permute-start(f32[8,96,128]{2,1,0:T(8,128)} %copy-done.123), channel_id=1, source_target_pairs={{0,1},{1,0},{2,3},{3,2},{4,5},{5,4},{6,7},{7,6},{8,9},{9,8},{10,11... | collective-permute-start | bytes 1179656 | tf_op jit(solution)/shard_map/ppermute | solution.py:589
  916.5 59.7 %collective-permute-start.93 = (f32[12,64,128]{2,1,0:T(8,128)S(1)}, f32[12,64,128]{2,1,0:T(8,128)S(1)}, u32[]{:S(2)}, u32[]{:S(2)}) collective-permute-start(f32[12,64,128]{2,1,0:T(8,128)S(1)} %get-tuple-element.243), channel_id=1, source_target_pairs={{0,8},{4,12},{8,0},{12,4},{16,24},{20,28},{24,16},{28,20},{1,9},{5... | collective-permute-start | bytes 1179656 | tf_op jit(solution)/shard_map/ppermute | solution.py:589
  946.4 86.8 %collective-permute-start.94 = (f32[12,64,128]{2,1,0:T(8,128)S(1)}, f32[12,64,128]{2,1,0:T(8,128)}, u32[]{:S(2)}, u32[]{:S(2)}) collective-permute-start(f32[12,64,128]{2,1,0:T(8,128)S(1)} %get-tuple-element.244), channel_id=1, source_target_pairs={{0,12},{4,8},{8,4},{12,0},{16,28},{20,24},{24,20},{28,16},{1,13},{... | collective-permute-start | bytes 1179656 | tf_op jit(solution)/shard_map/ppermute | solution.py:589
  946.4 86.8 %collective-permute-start.95 = (f32[12,64,128]{2,1,0:T(8,128)S(1)}, f32[12,64,128]{2,1,0:T(8,128)}, u32[]{:S(2)}, u32[]{:S(2)}) collective-permute-start(f32[12,64,128]{2,1,0:T(8,128)S(1)} %get-tuple-element.245), channel_id=1, source_target_pairs={{0,16},{4,20},{8,24},{12,28},{16,0},{20,4},{24,8},{28,12},{1,17},{... | collective-permute-start | bytes 1179656 | tf_op jit(solution)/shard_map/ppermute | solution.py:589
  957.9 75.3 %collective-permute-start.96 = (f32[12,64,128]{2,1,0:T(8,128)S(1)}, f32[12,64,128]{2,1,0:T(8,128)}, u32[]{:S(2)}, u32[]{:S(2)}) collective-permute-start(f32[12,64,128]{2,1,0:T(8,128)S(1)} %get-tuple-element.246), channel_id=1, source_target_pairs={{0,20},{4,16},{8,28},{12,24},{16,4},{20,0},{24,12},{28,8},{1,21},{... | collective-permute-start | bytes 1179656 | tf_op jit(solution)/shard_map/ppermute | solution.py:589
  974.2 59.0 %collective-permute-start.97 = (f32[12,64,128]{2,1,0:T(8,128)S(1)}, f32[12,64,128]{2,1,0:T(8,128)}, u32[]{:S(2)}, u32[]{:S(2)}) collective-permute-start(f32[12,64,128]{2,1,0:T(8,128)S(1)} %get-tuple-element.247), channel_id=1, source_target_pairs={{0,24},{4,28},{8,16},{12,20},{16,8},{20,12},{24,0},{28,4},{1,25},{... | collective-permute-start | bytes 1179656 | tf_op jit(solution)/shard_map/ppermute | solution.py:589
  (276 other events, 5964.0 us)
